TPU v7x, 128 devices: a whole 4x4x4 slice. The times are simulated.
128 devices in a mesh: seq: 16 (over y, x), exp: 8 (over z, core).
Axes of the slice: x: 4, y: 4, z: 4, core: 2. Of those that a mesh axis runs over, the one named last changes fastest.
Arguments:
- stream: bfloat16 [2048, 4096], P('seq', 'exp'), may hold values from -6 to 6
- mixer_in: bfloat16 [2048, 8192], P('seq', 'exp'), may hold values from -6 to 6
- gate_in: bfloat16 [2048, 8192], P('seq', 'exp'), may hold values from -6 to 6
- dt_raw: bfloat16 [2048, 8192], P('seq', 'exp'), may hold values from -2 to 13
- dt_bias: float32 [8192], P('exp'), may hold values from -13 to -2
- a_log: float32 [8192, 16], P('exp'), may hold values from -1.2 to 0.7
- conv_weight: float32 [8192, 4], P('exp'), may hold values from -3 to 3
- conv_bias: float32 [8192], P('exp'), may hold values from -6 to 6
- b_proj: float32 [2048, 16], P('seq'), may hold values from -6 to 6
- c_proj: float32 [2048, 16], P('seq'), may hold values from -6 to 6
- d_skip: float32 [8192], P('exp'), may hold values from 0.3 to 3
- w_out: bfloat16 [8192, 4096], P('exp', 'seq'), may hold values from -0.0625 to 0.0625
- expert_index: int32 [2048, 2], P('seq'), may hold values from 0 to 7, all different within a row; in each aligned block of 128 rows (0 to 127, 128 to 255, ...) at most 48 rows name the same one
- gate_weights: float32 [2048, 2], P('seq'), may hold values from 0.05 to 0.6
- norm_gain: float32 [4096], replicated, may hold values from 0.1 to 1.9
- w_gate: bfloat16 [8, 4096, 12288], P('exp', None, 'seq'), may hold values from -0.09375 to 0.09375
- w_up: bfloat16 [8, 4096, 12288], P('exp', None, 'seq'), may hold values from -0.09375 to 0.09375
- w_down: bfloat16 [8, 12288, 4096], P('exp', 'seq'), may hold values from -0.0546875 to 0.0546875
Outputs:
- block_out: bfloat16 [2048, 4096], P('seq', 'exp')
Inputs may be any that keep to these rules, and one draw needn't show every extreme that they name: `expert_index`: the two experts of a position differ. Among the 128 positions of one seq shard (aligned blocks), no expert is chosen by more than 48 routes, and in every draw some expert is chosen by exactly 48.
All inputs are finite; a program needn't handle non-finite values.
Results may differ from a plain program's by a relative error of at most 0.012.
Values may be sent and summed in bfloat16 or wider, within the bound.
No kernel may reach another device: no remote copies, remote signals or barrier semaphores. Data moves between devices by JAX's collectives and lax.ppermute only.
A program may use at most 192 MiB of HBM per device.

v0:
```python
import jax
import jax.numpy as jnp
from jax import lax
from jax.experimental import pallas as pl
from jax.experimental.pallas import tpu as pltpu
from jax.sharding import PartitionSpec as P

KCONV = 4
SIDE = 4
STATES = 16
LOG2E = 1.4426950408889634
F32 = jnp.float32
BF16 = jnp.bfloat16


def shift(value, axis, distance):
    cells = [(y, x) for y in range(SIDE) for x in range(SIDE)]
    if axis == "x":
        route = [(y * SIDE + x, y * SIDE + (x + distance) % SIDE) for y, x in cells]
    else:
        route = [(y * SIDE + x, (y + distance) % SIDE * SIDE + x) for y, x in cells]
    return lax.ppermute(value, "seq", route)


def partner(value):
    cells = range(SIDE * SIDE)
    return lax.ppermute(value, "seq", [(i, i ^ 1) for i in cells])


def ring_gather(block, axis):
    return [block] + [shift(block, axis, distance) for distance in range(1, SIDE)]


def relay_gather(blocks, axis):
    half = blocks.shape[0] // 2
    before = shift(blocks, axis, 1)
    after = shift(blocks, axis, -1)
    far = [shift(before[:half], axis, 1), shift(after[half:], axis, -1)]
    return [blocks, before, jnp.concatenate(far), after]


def grid_gather(block, order):
    near = jnp.stack(ring_gather(block, order[0]))
    return relay_gather(near, order[1])


def ring_scatter(blocks, axis):
    total = blocks[0].astype(F32)
    for k in (1, 3, 2):
        total = total + shift(blocks[k].astype(BF16), axis, -k).astype(F32)
    return total


def relay_scatter(blocks, axis):
    own, minus, far, plus = blocks
    half = far.shape[0] // 2
    via_plus = shift(far[:half], axis, 1).astype(F32)
    via_minus = shift(far[half:], axis, -1).astype(F32)
    plus = jnp.concatenate([(plus[:half].astype(F32) + via_plus).astype(BF16), plus[half:]])
    minus = jnp.concatenate([minus[:half], (minus[half:].astype(F32) + via_minus).astype(BF16)])
    total = own.astype(F32) + shift(plus, axis, 1).astype(F32)
    return total + shift(minus, axis, -1).astype(F32)


def fetch(sources, targets, semaphores):
    copies = [
        pltpu.make_async_copy(source, target, semaphores.at[i])
        for i, (source, target) in enumerate(zip(sources, targets))
    ]
    for copy in copies:
        copy.start()
    for copy in copies:
        copy.wait()


def copies_of(arrays):
    return [pltpu.VMEM(array.shape, array.dtype) for array in arrays] + [
        pltpu.SemaphoreType.DMA((len(arrays),))
    ]


def first_pass(x_hbm, dt_hbm, rim_ref, dtb_ref, cw_ref, cb_ref, rate_ref, b_ref,
               step_ref, act_ref, fin_ref, pad_ref, x_ref, dt_ref, semaphores):
    tokens, channels = x_ref.shape
    fetch((x_hbm, dt_hbm), (x_ref, dt_ref), semaphores)
    lanes = 128
    pad_ref[8 : 8 + tokens, :] = x_ref[...].astype(F32)
    pad_ref[0:8, :] = rim_ref[...].astype(F32)

    def columns(k, carry):
        cols = pl.ds(pl.multiple_of(k * lanes, lanes), lanes)
        total = cb_ref[:, cols]
        for tap in range(KCONV):
            low = 8 - (KCONV - 1) + tap
            total = total + cw_ref[tap : tap + 1, cols] * pad_ref[low : low + tokens, cols]
        act_ref[:, k, :] = total * jax.nn.sigmoid(total)
        raw = dt_ref[:, cols].astype(F32) + dtb_ref[:, cols]
        step_ref[:, k, :] = jnp.maximum(raw, 0.0) + jnp.log1p(jnp.exp(-jnp.abs(raw)))
        return carry

    lax.fori_loop(0, channels // lanes, columns, 0)

    def advance(t, carry):
        states, summed = carry
        step = step_ref[t]
        source = step * act_ref[t]
        states = tuple(
            jnp.exp2(step * rate_ref[n]) * states[n] + b_ref[t, n] * source for n in range(STATES)
        )
        return states, summed + step

    zero = jnp.zeros((8, lanes), F32)
    states, summed = lax.fori_loop(0, tokens, advance, ((zero,) * STATES, zero), unroll=2)
    for n in range(STATES):
        fin_ref[n] = states[n]
    fin_ref[STATES] = summed


def second_pass(step_hbm, act_hbm, gate_hbm, enter_ref, rate_ref, skip_ref, b_ref, c_ref,
                out_ref, y_ref, step_ref, act_ref, gate_ref, semaphores):
    tokens, channels = gate_ref.shape
    fetch((step_hbm, act_hbm, gate_hbm), (step_ref, act_ref, gate_ref), semaphores)
    lanes = 128
    skip = skip_ref[...]

    def advance(t, states):
        step = step_ref[t]
        act = act_ref[t]
        source = step * act
        sums = [skip * act, None]
        after = []
        for n in range(STATES):
            state = jnp.exp2(step * rate_ref[n]) * states[n] + b_ref[t, n] * source
            term = c_ref[t, n] * state
            sums[n % 2] = term if sums[n % 2] is None else sums[n % 2] + term
            after.append(state)
        y_ref[t] = sums[0] + sums[1]
        return tuple(after)

    lax.fori_loop(0, tokens, advance, tuple(enter_ref[n] for n in range(STATES)), unroll=2)

    def columns(k, carry):
        cols = pl.ds(pl.multiple_of(k * lanes, lanes), lanes)
        gate = gate_ref[:, cols].astype(F32)
        out_ref[:, cols] = (y_ref[:, k, :] * (gate * jax.nn.sigmoid(gate))).astype(BF16)
        return carry

    lax.fori_loop(0, channels // lanes, columns, 0)


def entering_state(final, rate, ahead, after):
    along_x = lax.axis_index("seq") % SIDE
    along_y = lax.axis_index("seq") // SIDE

    def chain(earlier, latter):
        decay = jnp.exp2(rate * latter[1])
        return decay * earlier[0] + latter[0], earlier[1] + latter[1]

    def masked(pair, reached):
        return jnp.where(reached, pair[0], 0.0), jnp.where(reached, pair[1], 0.0)

    def split(packed):
        return packed[:STATES], packed[STATES]

    def spread(packed, axis, place):
        others = [split(shift(packed, axis, d)) for d in range(1, SIDE)]
        before = masked(others[2], place >= 3)
        for d in (2, 1):
            before = chain(before, masked(others[d - 1], place >= d))
        return before, others

    own = split(final)
    before_x, others = spread(final, "x", along_x)
    total = chain(before_x, own)
    for d in (3, 2, 1):
        total = chain(total, masked(others[d - 1], along_x < d))
    packed = jnp.concatenate([total[0], total[1][None]], 0)
    packed, after = lax.optimization_barrier((packed, after))
    far = shift(after, "x", 2)
    packed, ahead = lax.optimization_barrier((packed, ahead))
    before_y, _ = spread(packed, "y", along_y)
    return chain(before_y, before_x)[0], ahead, [after, far]


def mixer(
    mixer_in, gate_in, dt_raw, dt_bias, a_log, conv_weight, conv_bias, b_proj, c_proj, d_skip, w_out
):
    tokens, channels = mixer_in.shape
    count, index = lax.axis_size("seq"), lax.axis_index("seq")
    rim = lax.ppermute(mixer_in[tokens - 8 :], "seq", [(i, i + 1) for i in range(count - 1)])
    split = 7 * channels // 16
    low, high = w_out[:split], w_out[split:]
    low_pair = jnp.stack([low, shift(low, "x", 2)])
    dt_raw, low_pair = lax.optimization_barrier((dt_raw, low_pair))
    high_ring = ring_gather(high, "y")
    rate = (-LOG2E * jnp.exp(a_log)).T.reshape(STATES, 8, 128)
    smem = pl.BlockSpec(memory_space=pltpu.SMEM)
    wide = jax.ShapeDtypeStruct((tokens, 8, 128), F32)
    ends = jax.ShapeDtypeStruct((STATES + 1, 8, 128), F32)
    vmem = pl.BlockSpec(memory_space=pltpu.VMEM)
    stay = pl.BlockSpec(memory_space=pltpu.HBM)
    step, act, final = pl.pallas_call(
        first_pass,
        out_shape=(wide, wide, ends),
        in_specs=[stay] * 2 + [vmem] * 5 + [smem],
        out_specs=[vmem] * 3,
        scratch_shapes=[pltpu.VMEM((tokens + 8, channels), F32), *copies_of((mixer_in, dt_raw))],
        compiler_params=pltpu.CompilerParams(vmem_limit_bytes=58 << 20),
        name="scan_state",
    )(mixer_in, dt_raw, rim, dt_bias[None, :], conv_weight.T, conv_bias[None, :], rate, b_proj)
    final, high_ring = lax.optimization_barrier((final, high_ring))
    first = ring_gather(low_pair, "y")
    high_ring = jnp.stack(high_ring)
    enter, first, second = entering_state(final, rate, first, high_ring)
    mixed = pl.pallas_call(
        second_pass,
        out_shape=jax.ShapeDtypeStruct((tokens, channels), BF16),
        in_specs=[stay] * 3 + [vmem] * 3 + [smem] * 2,
        out_specs=vmem,
        scratch_shapes=[pltpu.VMEM((tokens, 8, 128), F32), *copies_of((step, act, gate_in))],
        compiler_params=pltpu.CompilerParams(vmem_limit_bytes=58 << 20),
        name="scan_output",
    )(step, act, gate_in, enter, rate, d_skip.reshape(8, 128), b_proj, c_proj)
    return mixed, (first, second)


def project_kernel(place_ref, *refs):
    count = SIDE + 2
    keep_ref, send_ref, first, second, semaphores = refs[-5:]
    rows_ref, fixed = refs[count], refs[count + 1 : -5]
    targets = [first.at[i] for i in range(SIDE)] + [second.at[j] for j in range(2)]
    split = first.shape[2]
    y, side = place_ref[0], place_ref[1]

    def one(i, carry):
        plane = lax.rem(y - i + SIDE, SIDE)
        for j, ref in ((side, keep_ref), (1 - side, send_ref)):
            total = jnp.dot(rows_ref[:, :split], first[i, j], preferred_element_type=F32)
            total += jnp.dot(rows_ref[:, split:], second[j, i], preferred_element_type=F32)
            if fixed:
                ref[plane, 1] = total.astype(BF16)
            else:
                ref[plane] = total.astype(BF16)
        return carry

    fetch(refs[:count], targets, semaphores)
    if fixed:
        keep_ref[:, 0] = fixed[0][...]
        send_ref[:, 0] = fixed[1][...]
    lax.fori_loop(0, SIDE, one, 0)


def project(mixed, weights):
    first, second = weights
    tokens, columns = mixed.shape[0], first[0].shape[2]
    index, core = lax.axis_index("seq"), lax.axis_index("exp") % 2
    place = jnp.stack([index // SIDE, (core + index % SIDE // 2) % 2]).astype(jnp.int32)
    vmem = pl.BlockSpec(memory_space=pltpu.VMEM)
    stay = pl.BlockSpec(memory_space=pltpu.HBM)

    def call(shape, *operands):
        return pl.pallas_call(
            project_kernel,
            out_shape=[jax.ShapeDtypeStruct(shape, BF16)] * 2,
            in_specs=[pl.BlockSpec(memory_space=pltpu.SMEM)]
            + [stay] * (SIDE + 2)
            + [vmem] * len(operands),
            out_specs=[vmem] * 2,
            scratch_shapes=[
                pltpu.VMEM((SIDE, *first[0].shape), BF16),
                pltpu.VMEM((2, *second[0].shape), BF16),
                pltpu.SemaphoreType.DMA((SIDE + 2,)),
            ],
            compiler_params=pltpu.CompilerParams(vmem_limit_bytes=58 << 20),
            name="project",
        )(place, *first, *second, *operands)

    other = partner(mixed)
    own = call((SIDE, tokens, columns), mixed)
    keep, send = call((SIDE, 2, tokens, columns), other, *own)
    members = range(2 * SIDE)
    come = lax.ppermute(send, "exp", [(i, i ^ 1) for i in members])
    partial = (keep.astype(F32) + come.astype(F32)).astype(BF16)
    planes = [[i for i in members if i % 2 == c] for c in range(2)]
    partial = lax.all_to_all(
        partial, "exp", split_axis=0, concat_axis=0, axis_index_groups=planes
    )
    total = jnp.sum(partial.astype(F32), axis=0)
    other = partner(total[1].astype(BF16)).astype(F32)
    is_even = lax.axis_index("seq") % 2 == 0
    return jnp.concatenate(
        [jnp.where(is_even, total[0], other), jnp.where(is_even, other, total[0])], axis=1
    )


def local(
    stream,
    mixer_in,
    gate_in,
    dt_raw,
    dt_bias,
    a_log,
    conv_weight,
    conv_bias,
    b_proj,
    c_proj,
    d_skip,
    w_out,
    expert_index,
    gate_weights,
    norm_gain,
    w_gate,
    w_up,
    w_down,
):
    tokens = mixer_in.shape[0]
    experts = lax.axis_size("exp")
    groups = lax.axis_size("seq")
    capacity = 3 * tokens // experts
    width = stream.shape[1]
    mixed, weights = mixer(
        mixer_in, gate_in, dt_raw, dt_bias, a_log, conv_weight, conv_bias, b_proj, c_proj, d_skip, w_out
    )
    projected = project(mixed, weights)
    middle = (stream.astype(F32) + projected).astype(BF16)

    flat_exp = expert_index.reshape(-1)
    onehot = (flat_exp[:, None] == jnp.arange(experts, dtype=jnp.int32)[None, :]).astype(jnp.int32)
    ranks = jnp.cumsum(onehot, axis=0) - onehot
    slots = jnp.sum(ranks * onehot, axis=1)
    slot_id = (flat_exp * capacity + slots).reshape(tokens, 2)
    places = jnp.arange(experts * capacity, dtype=jnp.int32)
    chosen = (
        (slot_id[:, 0][None, :] == places[:, None]) | (slot_id[:, 1][None, :] == places[:, None])
    ).astype(BF16)
    outgoing = jnp.dot(chosen, middle, preferred_element_type=F32).astype(BF16)
    outgoing = outgoing.reshape(experts, capacity, width)
    arrived = lax.all_to_all(outgoing, "exp", split_axis=0, concat_axis=2, tiled=True)[0].astype(F32)
    mean_square = jnp.mean(arrived * arrived, axis=1, keepdims=True)
    normed = (arrived * lax.rsqrt(mean_square + 1e-05) * norm_gain[None, :]).astype(BF16)

    half = capacity // 2
    first = grid_gather(normed[:half], "xy")
    second = grid_gather(normed[half:], "yx")

    def feed(offsets):
        rows = jnp.stack([part[k] for part in (first, second) for k in offsets])
        flat = rows.reshape(-1, rows.shape[-1])
        gate_proj = jnp.dot(flat, w_gate[0], preferred_element_type=F32)
        up_proj = jnp.dot(flat, w_up[0], preferred_element_type=F32)
        hidden = lax.optimization_barrier((jax.nn.silu(gate_proj) * up_proj).astype(BF16))
        out = jnp.dot(hidden, w_down[0], preferred_element_type=F32).astype(BF16)
        return out.reshape((2, len(offsets)) + rows.shape[1:])

    fed = {}
    for offsets in ((0,), (1, 3), (2,)):
        out = feed(offsets)
        for at, k in enumerate(offsets):
            fed[k] = out[:, at]
    sums = []
    for which, order in ((0, "yx"), (1, "xy")):
        near = relay_scatter([fed[k][which] for k in range(SIDE)], order[0])
        sums.append(ring_scatter([near[k] for k in range(SIDE)], order[1]))
    summed = jnp.concatenate(sums, 0).astype(BF16)
    summed = summed.reshape(capacity, experts, width).transpose(1, 0, 2)
    returned = lax.all_to_all(summed, "exp", split_axis=0, concat_axis=0)
    returned = returned.reshape(experts * capacity, width)
    expert_sum = 0.0
    for k in range(2):
        pick = (slot_id[:, k][:, None] == places[None, :]).astype(BF16)
        picked = jnp.dot(pick, returned, preferred_element_type=F32)
        expert_sum = expert_sum + gate_weights[:, k][:, None] * picked
    return (middle.astype(F32) + expert_sum).astype(BF16)


def solution(mesh):
    return jax.shard_map(
        local,
        mesh=mesh,
        in_specs=(
            P("seq", "exp"),
            P("seq", "exp"),
            P("seq", "exp"),
            P("seq", "exp"),
            P("exp"),
            P("exp", None),
            P("exp", None),
            P("exp"),
            P("seq", None),
            P("seq", None),
            P("exp"),
            P("exp", "seq"),
            P("seq", None),
            P("seq", None),
            P(),
            P("exp", None, "seq"),
            P("exp", None, "seq"),
            P("exp", "seq", None),
        ),
        out_specs=P("seq", "exp"),
        check_vma=False,
    )
```

profile of v0, /device:TPU:1, one launch (start us, length us, event | category | flops | bytes accessed | tf_op | source)
XLA Modules:
  0.0 233.4 jit_solution(6136772368717316988)
XLA Ops:
  1.0 3.7 %collective-permute-start = (bf16[448,256]{1,0:T(8,128)(2,1)S(1)}, bf16[448,256]{1,0:T(8,128)(2,1)S(1)}, u32[]{:S(2)}, u32[]{:S(2)}) collective-permute-start(bf16[448,256]{1,0:T(8,128)(2,1)S(1)} %get-tuple-element.78), channel_id=1, source_target_pairs={{0,16},{8,24},{16,0},{24,8},{32,48},{40,56},{48,32},{56,40},{64,80... | collective-permute-start | bytes 688136 | tf_op jit(solution)/shard_map/ppermute | solution.py:22
  5.6 2.8 %collective-permute-start.4 = (bf16[576,256]{1,0:T(8,128)(2,1)S(1)}, bf16[576,256]{1,0:T(8,128)(2,1)S(1)}, u32[]{:S(2)}, u32[]{:S(2)}) collective-permute-start(bf16[576,256]{1,0:T(8,128)(2,1)S(1)} %slice.228), channel_id=1, source_target_pairs={{0,96},{8,104},{16,112},{24,120},{32,0},{40,8},{48,16},{56,24},{64... | collective-permute-start | bytes 884744 | tf_op jit(solution)/shard_map/ppermute | solution.py:22
  10.2 2.2 collective-permute-start.1
  15.4 2.1 collective-permute-start.10
  18.9 7.3 %scan_state.1 = (f32[128,8,128]{2,1,0:T(8,128)}, f32[128,8,128]{2,1,0:T(8,128)}, f32[17,8,128]{2,1,0:T(8,128)}) custom-call(bf16[128,1024]{1,0:T(8,128)(2,1)} %x_hbm.1, bf16[128,1024]{1,0:T(8,128)(2,1)} %dt_hbm, bf16[8,1024]{1,0:T(8,128)(2,1)} %copy-done.11, f32[1,1024]{1,0:T(1,128)} %bitcast.267, f32[4,1024]{1,0:T(4,128)} %bitcast.266, ...), custom_call_target="tpu_custom_call" | custom-call | tf_op jit(solution)/shard_map/scan_state/pallas_call | solution.py:202
  26.4 2.0 collective-permute-start.7
  29.2 1.5 collective-permute-done.7
  31.4 2.2 collective-permute-done.6
  35.3 7.3 %collective-permute-done.8.refs_1_ = bf16[2,448,256]{2,1,0:T(8,128)(2,1)S(1)} collective-permute-done((bf16[2,448,256]{2,1,0:T(8,128)(2,1)S(1)}, bf16[2,448,256]{2,1,0:T(8,128)(2,1)S(1)}, u32[]{:S(2)}, u32[]{:S(2)}) %collective-permute-start.8) | collective-permute-done | bytes 458784 | tf_op jit(solution)/shard_map/ppermute | solution.py:22
  44.7 1.5 collective-permute-start.14
  46.2 2.1 collective-permute-done.13
  48.4 2.5 %collective-permute-done.12 = f32[17,8,128]{2,1,0:T(8,128)S(1)} collective-permute-done((f32[17,8,128]{2,1,0:T(8,128)S(1)}, f32[17,8,128]{2,1,0:T(8,128)S(1)}, u32[]{:S(2)}, u32[]{:S(2)}) %collective-permute-start.12) | collective-permute-done | bytes 69664 | tf_op jit(solution)/shard_map/ppermute | solution.py:22
  51.6 8.5 %scan_output.1.refs_6_ = bf16[128,1024]{1,0:T(8,128)(2,1)} custom-call(f32[128,8,128]{2,1,0:T(8,128)} %get-tuple-element.40.step_hbm, f32[128,8,128]{2,1,0:T(8,128)} %get-tuple-element.41.act_hbm, bf16[128,1024]{1,0:T(8,128)(2,1)} %gate_hbm.1, f32[16,8,128]{2,1,0:T(8,128)} %fusion.67.enter_ref, f32[16,8,128]{2,1,0:T(8,128)} %bitcast.240, ...), custom_call_target="tpu_custom_call" | custom-call | tf_op jit(solution)/shard_map/scan_output/pallas_call | solution.py:215
  62.1 5.6 %project.2 = (bf16[4,128,256]{2,1,0:T(8,128)(2,1)}, bf16[4,128,256]{2,1,0:T(8,128)(2,1)}) custom-call(s32[2]{0:T(128)} %pad_add_fusion.place_ref, bf16[2,448,256]{2,1,0:T(8,128)(2,1)} %copy-done.2, bf16[2,448,256]{2,1,0:T(8,128)(2,1)} %copy-done.5, bf16[2,448,256]{2,1,0:T(8,128)(2,1)} %copy-done.4, bf16[2,448,256]{2,1,0:T(8,128)(2,1)} %copy-done.3, ...), custom_call_target="tpu_custom_call" | custom-call | tf_op jit(solution)/shard_map/project/pallas_call | solution.py:262
  68.4 6.0 %project.3 = (bf16[4,2,128,256]{3,2,1,0:T(8,128)(2,1)}, bf16[4,2,128,256]{3,2,1,0:T(8,128)(2,1)}) custom-call(s32[2]{0:T(128)} %pad_add_fusion.place_ref, bf16[2,448,256]{2,1,0:T(8,128)(2,1)} %copy-done.2, bf16[2,448,256]{2,1,0:T(8,128)(2,1)} %copy-done.5, bf16[2,448,256]{2,1,0:T(8,128)(2,1)} %copy-done.4, bf16[2,448,256]{2,1,0:T(8,128)(2,1)} %copy-done.3, ...), custom_call_target="tpu_custom_call" | custom-call | tf_op jit(solution)/shard_map/project/pallas_call | solution.py:262
  74.4 4.0 %collective-permute-start.16 = (bf16[4,2,128,256]{3,2,1,0:T(8,128)(2,1)}, bf16[4,2,128,256]{3,2,1,0:T(8,128)(2,1)S(1)}, u32[]{:S(2)}, u32[]{:S(2)}) collective-permute-start(bf16[4,2,128,256]{3,2,1,0:T(8,128)(2,1)} %get-tuple-element.46), channel_id=1, source_target_pairs={{0,1},{1,0},{2,3},{3,2},{4,5},{5,4},{6,7},{7,6},{8,9},{9,8},{10,11... | collective-permute-start | bytes 1572872 | tf_op jit(solution)/shard_map/ppermute | solution.py:282
  80.1 2.0 add_convert_fusion
  82.1 5.2 %all-to-all-start = ((bf16[4,2,128,256]{3,2,1,0:T(8,128)(2,1)}), bf16[4,2,128,256]{3,2,1,0:T(8,128)(2,1)S(1)}, u32[]{:S(2)}, u32[]{:S(2)}) async-start(bf16[4,2,128,256]{3,2,1,0:T(8,128)(2,1)} %add_convert_fusion), calls=%async_computation | async-start | bytes 1048576 | tf_op jit(solution)/shard_map/all_to_all | solution.py:285
  88.0 8.2 %all-to-all-done = bf16[4,2,128,256]{3,2,1,0:T(8,128)(2,1)S(1)} async-done(((bf16[4,2,128,256]{3,2,1,0:T(8,128)(2,1)}), bf16[4,2,128,256]{3,2,1,0:T(8,128)(2,1)S(1)}, u32[]{:S(2)}, u32[]{:S(2)}) %all-to-all-start) | async-done | bytes 524320 | tf_op jit(solution)/shard_map/all_to_all | solution.py:285
  97.5 2.0 collective-permute-done.17
  99.8 13.1 %all_to_all.19 = bf16[8,48,512]{2,1,0:T(8,128)(2,1)S(1)} all-to-all(bf16[8,48,512]{2,1,0:T(8,128)(2,1)S(1)} %bitcast.245), channel_id=1, replica_groups=mesh['seq'=16,'exp'=8] {'exp'}, dimensions={0} | all-to-all | bytes 786432 | tf_op jit(solution)/shard_map/all_to_all | solution.py:338
  114.6 2.2 collective-permute-start.21
  117.3 3.4 %collective-permute-start.19 = (bf16[24,4096]{1,0:T(8,128)(2,1)S(1)}, bf16[24,4096]{1,0:T(8,128)(2,1)S(1)}, u32[]{:S(2)}, u32[]{:S(2)}) collective-permute-start(bf16[24,4096]{1,0:T(8,128)(2,1)S(1)} %get-tuple-element.82), channel_id=1, source_target_pairs={{0,16},{8,24},{16,0},{24,8},{32,48},{40,56},{48,32},{56,40},{64,80... | collective-permute-start | bytes 589832 | tf_op jit(solution)/shard_map/ppermute | solution.py:22
  121.1 2.4 %collective-permute-start.20 = (bf16[24,4096]{1,0:T(8,128)(2,1)S(1)}, bf16[24,4096]{1,0:T(8,128)(2,1)S(1)}, u32[]{:S(2)}, u32[]{:S(2)}) collective-permute-start(bf16[24,4096]{1,0:T(8,128)(2,1)S(1)} %get-tuple-element.82), channel_id=1, source_target_pairs={{0,24},{8,0},{16,8},{24,16},{32,56},{40,32},{48,40},{56,48},{64,88... | collective-permute-start | bytes 589832 | tf_op jit(solution)/shard_map/ppermute | solution.py:22
  123.4 3.1 %collective-permute-done.21 = bf16[24,4096]{1,0:T(8,128)(2,1)S(1)} collective-permute-done((bf16[24,4096]{1,0:T(8,128)(2,1)S(1)}, bf16[24,4096]{1,0:T(8,128)(2,1)S(1)}, u32[]{:S(2)}, u32[]{:S(2)}) %collective-permute-start.21) | collective-permute-done | bytes 196640 | tf_op jit(solution)/shard_map/ppermute | solution.py:22
  127.8 1.6 collective-permute-start.27
  130.2 2.1 collective-permute-start.25
  135.2 1.4 fusion.38
  138.7 7.8 %collective-permute-done.26 = bf16[4,24,4096]{2,1,0:T(8,128)(2,1)S(1)} collective-permute-done((bf16[4,24,4096]{2,1,0:T(8,128)(2,1)S(1)}, bf16[4,24,4096]{2,1,0:T(8,128)(2,1)S(1)}, u32[]{:S(2)}, u32[]{:S(2)}) %collective-permute-start.26) | collective-permute-done | bytes 786464 | tf_op jit(solution)/shard_map/ppermute | solution.py:22
  147.5 1.9 collective-permute-start.31
  150.1 2.2 collective-permute-start.29
  152.7 2.6 %fusion.14 = f32[384,768]{1,0:T(8,128)S(1)} fusion(bf16[384,4096]{1,0:T(8,128)(2,1)S(1)} %bitcast.228, bf16[1,4096,768]{2,1,0:T(8,128)(2,1)S(1)} %bitcast.271), kind=kOutput, calls=%fused_computation.14 | convolution fusion | flops 2415919104 | bytes 10616832 | tf_op jit(solution)/shard_map/dot_general | solution.py:349
  155.3 2.7 %multiply_convert_fusion = bf16[384,768]{1,0:T(8,128)(2,1)S(1)} fusion(f32[384,768]{1,0:T(8,128)S(1)} %fusion.14, bf16[384,4096]{1,0:T(8,128)(2,1)S(1)} %bitcast.229, bf16[1,4096,768]{2,1,0:T(8,128)(2,1)S(1)} %bitcast.273), kind=kOutput, calls=%fused_computation.34 | convolution fusion | flops 2417688576 | bytes 11206656 | tf_op jit(solution)/shard_map/dot_general | solution.py:350
  158.0 2.8 %fusion.18 = bf16[384,4096]{1,0:T(8,128)(2,1)S(1)} fusion(bf16[384,768]{1,0:T(8,128)(2,1)S(1)} %multiply_convert_fusion, bf16[1,768,4096]{2,1,0:T(8,128)(2,1)S(1)} %bitcast.275), kind=kOutput, calls=%fused_computation.18 | convolution fusion | flops 2417491968 | bytes 10027008 | tf_op jit(solution)/shard_map/dot_general | solution.py:352
  162.6 1.4 fusion.35
  167.2 2.7 %collective-permute-start.34 = (bf16[2,24,4096]{2,1,0:T(8,128)(2,1)S(1)}, bf16[2,24,4096]{2,1,0:T(8,128)(2,1)S(1)}, u32[]{:S(2)}, u32[]{:S(2)}) collective-permute-start(bf16[2,24,4096]{2,1,0:T(8,128)(2,1)S(1)} %bitcast.251), channel_id=1, source_target_pairs={{0,96},{8,104},{16,112},{24,120},{32,0},{40,8},{48,16},{56,24},{64... | collective-permute-start | bytes 1179656 | tf_op jit(solution)/shard_map/ppermute | solution.py:22
  169.9 3.9 %collective-permute-done.41 = bf16[2,24,4096]{2,1,0:T(8,128)(2,1)S(1)} collective-permute-done((bf16[2,24,4096]{2,1,0:T(8,128)(2,1)S(1)}, bf16[2,24,4096]{2,1,0:T(8,128)(2,1)S(1)}, u32[]{:S(2)}, u32[]{:S(2)}) %collective-permute-start.41) | collective-permute-done | bytes 393248 | tf_op jit(solution)/shard_map/ppermute | solution.py:22
  177.0 1.7 collective-permute-start.42
  178.7 3.5 %collective-permute-start.35 = (bf16[4,24,4096]{2,1,0:T(8,128)(2,1)S(1)}, bf16[4,24,4096]{2,1,0:T(8,128)(2,1)S(1)}, u32[]{:S(2)}, u32[]{:S(2)}) collective-permute-start(bf16[4,24,4096]{2,1,0:T(8,128)(2,1)S(1)} %pad_maximum_fusion.7), channel_id=1, source_target_pairs={{0,96},{8,104},{16,112},{24,120},{32,0},{40,8},{48,16},{56,24},{64... | collective-permute-start | bytes 2359304 | tf_op jit(solution)/shard_map/ppermute | solution.py:22
  182.4 9.3 %collective-permute-done.40 = bf16[4,24,4096]{2,1,0:T(8,128)(2,1)S(1)} collective-permute-done((bf16[4,24,4096]{2,1,0:T(8,128)(2,1)S(1)}, bf16[4,24,4096]{2,1,0:T(8,128)(2,1)S(1)}, u32[]{:S(2)}, u32[]{:S(2)}) %collective-permute-start.40) | collective-permute-done | bytes 786464 | tf_op jit(solution)/shard_map/ppermute | solution.py:22
  192.7 2.8 %collective-permute-start.43 = (bf16[24,4096]{1,0:T(8,128)(2,1)S(1)}, bf16[24,4096]{1,0:T(8,128)(2,1)S(1)}, u32[]{:S(2)}, u32[]{:S(2)}) collective-permute-start(bf16[24,4096]{1,0:T(8,128)(2,1)S(1)} %get-tuple-element.70), channel_id=1, source_target_pairs={{0,96},{8,104},{16,112},{24,120},{32,0},{40,8},{48,16},{56,24},{64... | collective-permute-start | bytes 589832 | tf_op jit(solution)/shard_map/ppermute | solution.py:22
  197.9 1.4 collective-permute-start.36
  199.3 1.9 collective-permute-done.43
  201.3 2.3 collective-permute-done.45
  203.6 2.3 %collective-permute-done.44 = bf16[24,4096]{1,0:T(8,128)(2,1)S(1)} collective-permute-done((bf16[24,4096]{1,0:T(8,128)(2,1)S(1)}, bf16[24,4096]{1,0:T(8,128)(2,1)S(1)}, u32[]{:S(2)}, u32[]{:S(2)}) %collective-permute-start.44) | collective-permute-done | bytes 196640 | tf_op jit(solution)/shard_map/ppermute | solution.py:22
  206.1 1.6 collective-permute-done.37
  208.9 15.2 %all-to-all-start.2 = ((bf16[8,48,512]{2,1,0:T(8,128)(2,1)}), bf16[8,48,512]{2,1,0:T(8,128)(2,1)S(1)}, u32[]{:S(2)}, u32[]{:S(2)}) async-start(bf16[8,48,512]{2,1,0:T(8,128)(2,1)} %copy.55), calls=%async_computation.2 | async-start | bytes 786432 | tf_op jit(solution)/shard_map/all_to_all | solution.py:366
  224.1 8.1 %all-to-all-done.2 = bf16[8,48,512]{2,1,0:T(8,128)(2,1)S(1)} async-done(((bf16[8,48,512]{2,1,0:T(8,128)(2,1)}), bf16[8,48,512]{2,1,0:T(8,128)(2,1)S(1)}, u32[]{:S(2)}, u32[]{:S(2)}) %all-to-all-start.2) | async-done | bytes 393248 | tf_op jit(solution)/shard_map/all_to_all | solution.py:366
  (179 shorter events, 46.6 us)
Async XLA Ops:
  1.0 14.4 %collective-permute-start = (bf16[448,256]{1,0:T(8,128)(2,1)S(1)}, bf16[448,256]{1,0:T(8,128)(2,1)S(1)}, u32[]{:S(2)}, u32[]{:S(2)}) collective-permute-start(bf16[448,256]{1,0:T(8,128)(2,1)S(1)} %get-tuple-element.78), channel_id=1, source_target_pairs={{0,16},{8,24},{16,0},{24,8},{32,48},{40,56},{48,32},{56,40},{64,80... | collective-permute-start | bytes 688136 | tf_op jit(solution)/shard_map/ppermute | solution.py:22
  5.6 20.6 %collective-permute-start.4 = (bf16[576,256]{1,0:T(8,128)(2,1)S(1)}, bf16[576,256]{1,0:T(8,128)(2,1)S(1)}, u32[]{:S(2)}, u32[]{:S(2)}) collective-permute-start(bf16[576,256]{1,0:T(8,128)(2,1)S(1)} %slice.228), channel_id=1, source_target_pairs={{0,96},{8,104},{16,112},{24,120},{32,0},{40,8},{48,16},{56,24},{64... | collective-permute-start | bytes 884744 | tf_op jit(solution)/shard_map/ppermute | solution.py:22
  8.4 17.8 %collective-permute-start.3 = (bf16[576,256]{1,0:T(8,128)(2,1)S(1)}, bf16[576,256]{1,0:T(8,128)(2,1)S(1)}, u32[]{:S(2)}, u32[]{:S(2)}) collective-permute-start(bf16[576,256]{1,0:T(8,128)(2,1)S(1)} %slice.228), channel_id=1, source_target_pairs={{0,64},{8,72},{16,80},{24,88},{32,96},{40,104},{48,112},{56,120},{... | collective-permute-start | bytes 884744 | tf_op jit(solution)/shard_map/ppermute | solution.py:22
  8.8 17.7 %collective-permute-start.2 = (bf16[576,256]{1,0:T(8,128)(2,1)S(1)}, bf16[576,256]{1,0:T(8,128)(2,1)S(1)}, u32[]{:S(2)}, u32[]{:S(2)}) collective-permute-start(bf16[576,256]{1,0:T(8,128)(2,1)S(1)} %slice.228), channel_id=1, source_target_pairs={{0,32},{8,40},{16,48},{24,56},{32,64},{40,72},{48,80},{56,88},{64,... | collective-permute-start | bytes 884744 | tf_op jit(solution)/shard_map/ppermute | solution.py:22
  10.2 7.3 %collective-permute-start.1 = (bf16[8,1024]{1,0:T(8,128)(2,1)S(1)}, bf16[8,1024]{1,0:T(8,128)(2,1)S(1)}, u32[]{:S(2)}, u32[]{:S(2)}) collective-permute-start(bf16[8,1024]{1,0:T(8,128)(2,1)S(1)} %slice.227), channel_id=1, source_target_pairs={{0,8},{8,16},{16,24},{24,32},{32,40},{40,48},{48,56},{56,64},{64,7... | collective-permute-start | bytes 49160 | tf_op jit(solution)/shard_map/ppermute | solution.py:190
  15.4 19.9 %collective-permute-start.10 = (bf16[2,448,256]{2,1,0:T(8,128)(2,1)S(1)}, bf16[2,448,256]{2,1,0:T(8,128)(2,1)S(1)}, u32[]{:S(2)}, u32[]{:S(2)}) collective-permute-start(bf16[2,448,256]{2,1,0:T(8,128)(2,1)S(1)} %pad_maximum_fusion.10.refs_0_), channel_id=1, source_target_pairs={{0,96},{8,104},{16,112},{24,120},{32,0},{40,8},{48,16},{56,24},{64... | collective-permute-start | bytes 1376264 | tf_op jit(solution)/shard_map/ppermute | solution.py:22
  17.5 17.8 %collective-permute-start.9 = (bf16[2,448,256]{2,1,0:T(8,128)(2,1)S(1)}, bf16[2,448,256]{2,1,0:T(8,128)(2,1)S(1)}, u32[]{:S(2)}, u32[]{:S(2)}) collective-permute-start(bf16[2,448,256]{2,1,0:T(8,128)(2,1)S(1)} %pad_maximum_fusion.10.refs_0_), channel_id=1, source_target_pairs={{0,64},{8,72},{16,80},{24,88},{32,96},{40,104},{48,112},{56,120},{... | collective-permute-start | bytes 1376264 | tf_op jit(solution)/shard_map/ppermute | solution.py:22
  26.4 4.3 %collective-permute-start.7 = (f32[17,8,128]{2,1,0:T(8,128)}, f32[17,8,128]{2,1,0:T(8,128)S(1)}, u32[]{:S(2)}, u32[]{:S(2)}) collective-permute-start(f32[17,8,128]{2,1,0:T(8,128)} %get-tuple-element.28), channel_id=1, source_target_pairs={{0,24},{8,0},{16,8},{24,16},{32,56},{40,32},{48,40},{56,48},{64,88... | collective-permute-start | bytes 208904 | tf_op jit(solution)/shard_map/ppermute | solution.py:22
  28.4 5.2 %collective-permute-start.6 = (f32[17,8,128]{2,1,0:T(8,128)}, f32[17,8,128]{2,1,0:T(8,128)S(1)}, u32[]{:S(2)}, u32[]{:S(2)}) collective-permute-start(f32[17,8,128]{2,1,0:T(8,128)} %get-tuple-element.28), channel_id=1, source_target_pairs={{0,16},{8,24},{16,0},{24,8},{32,48},{40,56},{48,32},{56,40},{64,80... | collective-permute-start | bytes 208904 | tf_op jit(solution)/shard_map/ppermute | solution.py:22
  28.9 5.5 %collective-permute-start.5 = (f32[17,8,128]{2,1,0:T(8,128)}, f32[17,8,128]{2,1,0:T(8,128)S(1)}, u32[]{:S(2)}, u32[]{:S(2)}) collective-permute-start(f32[17,8,128]{2,1,0:T(8,128)} %get-tuple-element.28), channel_id=1, source_target_pairs={{0,8},{8,16},{16,24},{24,0},{32,40},{40,48},{48,56},{56,32},{64,72... | collective-permute-start | bytes 208904 | tf_op jit(solution)/shard_map/ppermute | solution.py:22
  30.8 11.9 %collective-permute-start.8 = (bf16[2,448,256]{2,1,0:T(8,128)(2,1)S(1)}, bf16[2,448,256]{2,1,0:T(8,128)(2,1)S(1)}, u32[]{:S(2)}, u32[]{:S(2)}) collective-permute-start(bf16[2,448,256]{2,1,0:T(8,128)(2,1)S(1)} %pad_maximum_fusion.10.refs_0_), channel_id=1, source_target_pairs={{0,32},{8,40},{16,48},{24,56},{32,64},{40,72},{48,80},{56,88},{64,... | collective-permute-start | bytes 1376264 | tf_op jit(solution)/shard_map/ppermute | solution.py:22
  34.5 26.6 %collective-permute-start.11 = (bf16[4,576,256]{2,1,0:T(8,128)(2,1)S(1)}, bf16[4,576,256]{2,1,0:T(8,128)(2,1)S(1)}, u32[]{:S(2)}, u32[]{:S(2)}) collective-permute-start(bf16[4,576,256]{2,1,0:T(8,128)(2,1)S(1)} %pad_maximum_fusion.3.refs_4_), channel_id=1, source_target_pairs={{0,16},{8,24},{16,0},{24,8},{32,48},{40,56},{48,32},{56,40},{64,80... | collective-permute-start | bytes 3538952 | tf_op jit(solution)/shard_map/ppermute | solution.py:22
  43.4 5.0 %collective-permute-start.13 = (f32[17,8,128]{2,1,0:T(8,128)S(1)}, f32[17,8,128]{2,1,0:T(8,128)S(1)}, u32[]{:S(2)}, u32[]{:S(2)}) collective-permute-start(f32[17,8,128]{2,1,0:T(8,128)S(1)} %pad_maximum_fusion.11), channel_id=1, source_target_pairs={{0,64},{8,72},{16,80},{24,88},{32,96},{40,104},{48,112},{56,120},{... | collective-permute-start | bytes 208904 | tf_op jit(solution)/shard_map/ppermute | solution.py:22
  44.7 6.2 %collective-permute-start.14 = (f32[17,8,128]{2,1,0:T(8,128)S(1)}, f32[17,8,128]{2,1,0:T(8,128)S(1)}, u32[]{:S(2)}, u32[]{:S(2)}) collective-permute-start(f32[17,8,128]{2,1,0:T(8,128)S(1)} %pad_maximum_fusion.11), channel_id=1, source_target_pairs={{0,96},{8,104},{16,112},{24,120},{32,0},{40,8},{48,16},{56,24},{64... | collective-permute-start | bytes 208904 | tf_op jit(solution)/shard_map/ppermute | solution.py:22
  46.2 4.7 %collective-permute-start.12 = (f32[17,8,128]{2,1,0:T(8,128)S(1)}, f32[17,8,128]{2,1,0:T(8,128)S(1)}, u32[]{:S(2)}, u32[]{:S(2)}) collective-permute-start(f32[17,8,128]{2,1,0:T(8,128)S(1)} %pad_maximum_fusion.11), channel_id=1, source_target_pairs={{0,32},{8,40},{16,48},{24,56},{32,64},{40,72},{48,80},{56,88},{64,... | collective-permute-start | bytes 208904 | tf_op jit(solution)/shard_map/ppermute | solution.py:22
  60.1 7.6 %collective-permute-start.15 = (bf16[128,1024]{1,0:T(8,128)(2,1)}, bf16[128,1024]{1,0:T(8,128)(2,1)S(1)}, u32[]{:S(2)}, u32[]{:S(2)}) collective-permute-start(bf16[128,1024]{1,0:T(8,128)(2,1)} %scan_output.1.refs_6_), channel_id=1, source_target_pairs={{0,8},{8,0},{16,24},{24,16},{32,40},{40,32},{48,56},{56,48},{64,72... | collective-permute-start | bytes 786440 | tf_op jit(solution)/shard_map/ppermute | solution.py:27
  74.4 5.7 %collective-permute-start.16 = (bf16[4,2,128,256]{3,2,1,0:T(8,128)(2,1)}, bf16[4,2,128,256]{3,2,1,0:T(8,128)(2,1)S(1)}, u32[]{:S(2)}, u32[]{:S(2)}) collective-permute-start(bf16[4,2,128,256]{3,2,1,0:T(8,128)(2,1)} %get-tuple-element.46), channel_id=1, source_target_pairs={{0,1},{1,0},{2,3},{3,2},{4,5},{5,4},{6,7},{7,6},{8,9},{9,8},{10,11... | collective-permute-start | bytes 1572872 | tf_op jit(solution)/shard_map/ppermute | solution.py:282
  82.1 14.1 %all-to-all-start = ((bf16[4,2,128,256]{3,2,1,0:T(8,128)(2,1)}), bf16[4,2,128,256]{3,2,1,0:T(8,128)(2,1)S(1)}, u32[]{:S(2)}, u32[]{:S(2)}) async-start(bf16[4,2,128,256]{3,2,1,0:T(8,128)(2,1)} %add_convert_fusion), calls=%async_computation | async-start | bytes 1048576 | tf_op jit(solution)/shard_map/all_to_all | solution.py:285
  96.3 3.2 %collective-permute-start.17 = (bf16[128,256]{1,0:T(8,128)(2,1)S(1)}, bf16[128,256]{1,0:T(8,128)(2,1)S(1)}, u32[]{:S(2)}, u32[]{:S(2)}) collective-permute-start(bf16[128,256]{1,0:T(8,128)(2,1)S(1)} %fusion.64), channel_id=1, source_target_pairs={{0,8},{8,0},{16,24},{24,16},{32,40},{40,32},{48,56},{56,48},{64,72... | collective-permute-start | bytes 196616 | tf_op jit(solution)/shard_map/ppermute | solution.py:27
  113.9 7.2 %collective-permute-start.22 = (bf16[24,4096]{1,0:T(8,128)(2,1)S(1)}, bf16[24,4096]{1,0:T(8,128)(2,1)S(1)}, u32[]{:S(2)}, u32[]{:S(2)}) collective-permute-start(bf16[24,4096]{1,0:T(8,128)(2,1)S(1)} %get-tuple-element.81), channel_id=1, source_target_pairs={{0,64},{8,72},{16,80},{24,88},{32,96},{40,104},{48,112},{56,120},{... | collective-permute-start | bytes 589832 | tf_op jit(solution)/shard_map/ppermute | solution.py:22
  114.6 11.9 %collective-permute-start.21 = (bf16[24,4096]{1,0:T(8,128)(2,1)S(1)}, bf16[24,4096]{1,0:T(8,128)(2,1)S(1)}, u32[]{:S(2)}, u32[]{:S(2)}) collective-permute-start(bf16[24,4096]{1,0:T(8,128)(2,1)S(1)} %get-tuple-element.81), channel_id=1, source_target_pairs={{0,32},{8,40},{16,48},{24,56},{32,64},{40,72},{48,80},{56,88},{64,... | collective-permute-start | bytes 589832 | tf_op jit(solution)/shard_map/ppermute | solution.py:22
  116.8 9.7 %collective-permute-start.23 = (bf16[24,4096]{1,0:T(8,128)(2,1)S(1)}, bf16[24,4096]{1,0:T(8,128)(2,1)S(1)}, u32[]{:S(2)}, u32[]{:S(2)}) collective-permute-start(bf16[24,4096]{1,0:T(8,128)(2,1)S(1)} %get-tuple-element.81), channel_id=1, source_target_pairs={{0,96},{8,104},{16,112},{24,120},{32,0},{40,8},{48,16},{56,24},{64... | collective-permute-start | bytes 589832 | tf_op jit(solution)/shard_map/ppermute | solution.py:22
  117.3 12.1 %collective-permute-start.19 = (bf16[24,4096]{1,0:T(8,128)(2,1)S(1)}, bf16[24,4096]{1,0:T(8,128)(2,1)S(1)}, u32[]{:S(2)}, u32[]{:S(2)}) collective-permute-start(bf16[24,4096]{1,0:T(8,128)(2,1)S(1)} %get-tuple-element.82), channel_id=1, source_target_pairs={{0,16},{8,24},{16,0},{24,8},{32,48},{40,56},{48,32},{56,40},{64,80... | collective-permute-start | bytes 589832 | tf_op jit(solution)/shard_map/ppermute | solution.py:22
  120.8 8.6 %collective-permute-start.18 = (bf16[24,4096]{1,0:T(8,128)(2,1)S(1)}, bf16[24,4096]{1,0:T(8,128)(2,1)S(1)}, u32[]{:S(2)}, u32[]{:S(2)}) collective-permute-start(bf16[24,4096]{1,0:T(8,128)(2,1)S(1)} %get-tuple-element.82), channel_id=1, source_target_pairs={{0,8},{8,16},{16,24},{24,0},{32,40},{40,48},{48,56},{56,32},{64,72... | collective-permute-start | bytes 589832 | tf_op jit(solution)/shard_map/ppermute | solution.py:22
  121.1 8.3 %collective-permute-start.20 = (bf16[24,4096]{1,0:T(8,128)(2,1)S(1)}, bf16[24,4096]{1,0:T(8,128)(2,1)S(1)}, u32[]{:S(2)}, u32[]{:S(2)}) collective-permute-start(bf16[24,4096]{1,0:T(8,128)(2,1)S(1)} %get-tuple-element.82), channel_id=1, source_target_pairs={{0,24},{8,0},{16,8},{24,16},{32,56},{40,32},{48,40},{56,48},{64,88... | collective-permute-start | bytes 589832 | tf_op jit(solution)/shard_map/ppermute | solution.py:22
  126.6 19.9 %collective-permute-start.26 = (bf16[4,24,4096]{2,1,0:T(8,128)(2,1)S(1)}, bf16[4,24,4096]{2,1,0:T(8,128)(2,1)S(1)}, u32[]{:S(2)}, u32[]{:S(2)}) collective-permute-start(bf16[4,24,4096]{2,1,0:T(8,128)(2,1)S(1)} %get-tuple-element.76), channel_id=1, source_target_pairs={{0,8},{8,16},{16,24},{24,0},{32,40},{40,48},{48,56},{56,32},{64,72... | collective-permute-start | bytes 2359304 | tf_op jit(solution)/shard_map/ppermute | solution.py:22
  127.8 19.7 %collective-permute-start.27 = (bf16[4,24,4096]{2,1,0:T(8,128)(2,1)S(1)}, bf16[4,24,4096]{2,1,0:T(8,128)(2,1)S(1)}, u32[]{:S(2)}, u32[]{:S(2)}) collective-permute-start(bf16[4,24,4096]{2,1,0:T(8,128)(2,1)S(1)} %get-tuple-element.76), channel_id=1, source_target_pairs={{0,24},{8,0},{16,8},{24,16},{32,56},{40,32},{48,40},{56,48},{64,88... | collective-permute-start | bytes 2359304 | tf_op jit(solution)/shard_map/ppermute | solution.py:22
  129.5 19.9 %collective-permute-start.24 = (bf16[4,24,4096]{2,1,0:T(8,128)(2,1)S(1)}, bf16[4,24,4096]{2,1,0:T(8,128)(2,1)S(1)}, u32[]{:S(2)}, u32[]{:S(2)}) collective-permute-start(bf16[4,24,4096]{2,1,0:T(8,128)(2,1)S(1)} %get-tuple-element.74), channel_id=1, source_target_pairs={{0,32},{8,40},{16,48},{24,56},{32,64},{40,72},{48,80},{56,88},{64,... | collective-permute-start | bytes 2359304 | tf_op jit(solution)/shard_map/ppermute | solution.py:22
  130.2 19.9 %collective-permute-start.25 = (bf16[4,24,4096]{2,1,0:T(8,128)(2,1)S(1)}, bf16[4,24,4096]{2,1,0:T(8,128)(2,1)S(1)}, u32[]{:S(2)}, u32[]{:S(2)}) collective-permute-start(bf16[4,24,4096]{2,1,0:T(8,128)(2,1)S(1)} %get-tuple-element.74), channel_id=1, source_target_pairs={{0,96},{8,104},{16,112},{24,120},{32,0},{40,8},{48,16},{56,24},{64... | collective-permute-start | bytes 2359304 | tf_op jit(solution)/shard_map/ppermute | solution.py:22
  146.6 14.2 %collective-permute-start.30 = (bf16[2,24,4096]{2,1,0:T(8,128)(2,1)S(1)}, bf16[2,24,4096]{2,1,0:T(8,128)(2,1)S(1)}, u32[]{:S(2)}, u32[]{:S(2)}) collective-permute-start(bf16[2,24,4096]{2,1,0:T(8,128)(2,1)S(1)} %slice.306), channel_id=1, source_target_pairs={{0,8},{8,16},{16,24},{24,0},{32,40},{40,48},{48,56},{56,32},{64,72... | collective-permute-start | bytes 1179656 | tf_op jit(solution)/shard_map/ppermute | solution.py:22
  147.5 13.3 %collective-permute-start.31 = (bf16[2,24,4096]{2,1,0:T(8,128)(2,1)S(1)}, bf16[2,24,4096]{2,1,0:T(8,128)(2,1)S(1)}, u32[]{:S(2)}, u32[]{:S(2)}) collective-permute-start(bf16[2,24,4096]{2,1,0:T(8,128)(2,1)S(1)} %slice.307), channel_id=1, source_target_pairs={{0,24},{8,0},{16,8},{24,16},{32,56},{40,32},{48,40},{56,48},{64,88... | collective-permute-start | bytes 1179656 | tf_op jit(solution)/shard_map/ppermute | solution.py:22
  149.5 11.5 %collective-permute-start.28 = (bf16[2,24,4096]{2,1,0:T(8,128)(2,1)S(1)}, bf16[2,24,4096]{2,1,0:T(8,128)(2,1)S(1)}, u32[]{:S(2)}, u32[]{:S(2)}) collective-permute-start(bf16[2,24,4096]{2,1,0:T(8,128)(2,1)S(1)} %slice.304), channel_id=1, source_target_pairs={{0,32},{8,40},{16,48},{24,56},{32,64},{40,72},{48,80},{56,88},{64,... | collective-permute-start | bytes 1179656 | tf_op jit(solution)/shard_map/ppermute | solution.py:22
  150.1 10.8 %collective-permute-start.29 = (bf16[2,24,4096]{2,1,0:T(8,128)(2,1)S(1)}, bf16[2,24,4096]{2,1,0:T(8,128)(2,1)S(1)}, u32[]{:S(2)}, u32[]{:S(2)}) collective-permute-start(bf16[2,24,4096]{2,1,0:T(8,128)(2,1)S(1)} %slice.305), channel_id=1, source_target_pairs={{0,96},{8,104},{16,112},{24,120},{32,0},{40,8},{48,16},{56,24},{64... | collective-permute-start | bytes 1179656 | tf_op jit(solution)/shard_map/ppermute | solution.py:22
  165.6 8.2 %collective-permute-start.41 = (bf16[2,24,4096]{2,1,0:T(8,128)(2,1)S(1)}, bf16[2,24,4096]{2,1,0:T(8,128)(2,1)S(1)}, u32[]{:S(2)}, u32[]{:S(2)}) collective-permute-start(bf16[2,24,4096]{2,1,0:T(8,128)(2,1)S(1)} %bitcast.254), channel_id=1, source_target_pairs={{0,24},{8,0},{16,8},{24,16},{32,56},{40,32},{48,40},{56,48},{64,88... | collective-permute-start | bytes 1179656 | tf_op jit(solution)/shard_map/ppermute | solution.py:22
  166.0 7.9 %collective-permute-start.32 = (bf16[2,24,4096]{2,1,0:T(8,128)(2,1)S(1)}, bf16[2,24,4096]{2,1,0:T(8,128)(2,1)S(1)}, u32[]{:S(2)}, u32[]{:S(2)}) collective-permute-start(bf16[2,24,4096]{2,1,0:T(8,128)(2,1)S(1)} %bitcast.253), channel_id=1, source_target_pairs={{0,32},{8,40},{16,48},{24,56},{32,64},{40,72},{48,80},{56,88},{64,... | collective-permute-start | bytes 1179656 | tf_op jit(solution)/shard_map/ppermute | solution.py:22
  166.0 7.9 %collective-permute-start.39 = (bf16[2,24,4096]{2,1,0:T(8,128)(2,1)S(1)}, bf16[2,24,4096]{2,1,0:T(8,128)(2,1)S(1)}, u32[]{:S(2)}, u32[]{:S(2)}) collective-permute-start(bf16[2,24,4096]{2,1,0:T(8,128)(2,1)S(1)} %bitcast.252), channel_id=1, source_target_pairs={{0,8},{8,16},{16,24},{24,0},{32,40},{40,48},{48,56},{56,32},{64,72... | collective-permute-start | bytes 1179656 | tf_op jit(solution)/shard_map/ppermute | solution.py:22
  167.2 7.8 %collective-permute-start.34 = (bf16[2,24,4096]{2,1,0:T(8,128)(2,1)S(1)}, bf16[2,24,4096]{2,1,0:T(8,128)(2,1)S(1)}, u32[]{:S(2)}, u32[]{:S(2)}) collective-permute-start(bf16[2,24,4096]{2,1,0:T(8,128)(2,1)S(1)} %bitcast.251), channel_id=1, source_target_pairs={{0,96},{8,104},{16,112},{24,120},{32,0},{40,8},{48,16},{56,24},{64... | collective-permute-start | bytes 1179656 | tf_op jit(solution)/shard_map/ppermute | solution.py:22
  175.6 16.1 %collective-permute-start.40 = (bf16[4,24,4096]{2,1,0:T(8,128)(2,1)S(1)}, bf16[4,24,4096]{2,1,0:T(8,128)(2,1)S(1)}, u32[]{:S(2)}, u32[]{:S(2)}) collective-permute-start(bf16[4,24,4096]{2,1,0:T(8,128)(2,1)S(1)} %pad_maximum_fusion.8), channel_id=1, source_target_pairs={{0,8},{8,16},{16,24},{24,0},{32,40},{40,48},{48,56},{56,32},{64,72... | collective-permute-start | bytes 2359304 | tf_op jit(solution)/shard_map/ppermute | solution.py:22
  177.0 15.4 %collective-permute-start.42 = (bf16[4,24,4096]{2,1,0:T(8,128)(2,1)S(1)}, bf16[4,24,4096]{2,1,0:T(8,128)(2,1)S(1)}, u32[]{:S(2)}, u32[]{:S(2)}) collective-permute-start(bf16[4,24,4096]{2,1,0:T(8,128)(2,1)S(1)} %pad_maximum_fusion.9), channel_id=1, source_target_pairs={{0,24},{8,0},{16,8},{24,16},{32,56},{40,32},{48,40},{56,48},{64,88... | collective-permute-start | bytes 2359304 | tf_op jit(solution)/shard_map/ppermute | solution.py:22
  178.7 17.4 %collective-permute-start.35 = (bf16[4,24,4096]{2,1,0:T(8,128)(2,1)S(1)}, bf16[4,24,4096]{2,1,0:T(8,128)(2,1)S(1)}, u32[]{:S(2)}, u32[]{:S(2)}) collective-permute-start(bf16[4,24,4096]{2,1,0:T(8,128)(2,1)S(1)} %pad_maximum_fusion.7), channel_id=1, source_target_pairs={{0,96},{8,104},{16,112},{24,120},{32,0},{40,8},{48,16},{56,24},{64... | collective-permute-start | bytes 2359304 | tf_op jit(solution)/shard_map/ppermute | solution.py:22
  182.3 15.3 %collective-permute-start.33 = (bf16[4,24,4096]{2,1,0:T(8,128)(2,1)S(1)}, bf16[4,24,4096]{2,1,0:T(8,128)(2,1)S(1)}, u32[]{:S(2)}, u32[]{:S(2)}) collective-permute-start(bf16[4,24,4096]{2,1,0:T(8,128)(2,1)S(1)} %pad_maximum_fusion.6), channel_id=1, source_target_pairs={{0,32},{8,40},{16,48},{24,56},{32,64},{40,72},{48,80},{56,88},{64,... | collective-permute-start | bytes 2359304 | tf_op jit(solution)/shard_map/ppermute | solution.py:22
  192.7 8.5 %collective-permute-start.43 = (bf16[24,4096]{1,0:T(8,128)(2,1)S(1)}, bf16[24,4096]{1,0:T(8,128)(2,1)S(1)}, u32[]{:S(2)}, u32[]{:S(2)}) collective-permute-start(bf16[24,4096]{1,0:T(8,128)(2,1)S(1)} %get-tuple-element.70), channel_id=1, source_target_pairs={{0,96},{8,104},{16,112},{24,120},{32,0},{40,8},{48,16},{56,24},{64... | collective-permute-start | bytes 589832 | tf_op jit(solution)/shard_map/ppermute | solution.py:22
  195.5 8.1 %collective-permute-start.45 = (bf16[24,4096]{1,0:T(8,128)(2,1)S(1)}, bf16[24,4096]{1,0:T(8,128)(2,1)S(1)}, u32[]{:S(2)}, u32[]{:S(2)}) collective-permute-start(bf16[24,4096]{1,0:T(8,128)(2,1)S(1)} %get-tuple-element.71), channel_id=1, source_target_pairs={{0,64},{8,72},{16,80},{24,88},{32,96},{40,104},{48,112},{56,120},{... | collective-permute-start | bytes 589832 | tf_op jit(solution)/shard_map/ppermute | solution.py:22
  195.5 10.4 %collective-permute-start.44 = (bf16[24,4096]{1,0:T(8,128)(2,1)S(1)}, bf16[24,4096]{1,0:T(8,128)(2,1)S(1)}, u32[]{:S(2)}, u32[]{:S(2)}) collective-permute-start(bf16[24,4096]{1,0:T(8,128)(2,1)S(1)} %get-tuple-element.72), channel_id=1, source_target_pairs={{0,32},{8,40},{16,48},{24,56},{32,64},{40,72},{48,80},{56,88},{64,... | collective-permute-start | bytes 589832 | tf_op jit(solution)/shard_map/ppermute | solution.py:22
  197.9 8.2 %collective-permute-start.36 = (bf16[24,4096]{1,0:T(8,128)(2,1)S(1)}, bf16[24,4096]{1,0:T(8,128)(2,1)S(1)}, u32[]{:S(2)}, u32[]{:S(2)}) collective-permute-start(bf16[24,4096]{1,0:T(8,128)(2,1)S(1)} %get-tuple-element.67), channel_id=1, source_target_pairs={{0,24},{8,0},{16,8},{24,16},{32,56},{40,32},{48,40},{56,48},{64,88... | collective-permute-start | bytes 589832 | tf_op jit(solution)/shard_map/ppermute | solution.py:22
  199.3 6.8 %collective-permute-start.38 = (bf16[24,4096]{1,0:T(8,128)(2,1)S(1)}, bf16[24,4096]{1,0:T(8,128)(2,1)S(1)}, u32[]{:S(2)}, u32[]{:S(2)}) collective-permute-start(bf16[24,4096]{1,0:T(8,128)(2,1)S(1)} %get-tuple-element.68), channel_id=1, source_target_pairs={{0,16},{8,24},{16,0},{24,8},{32,48},{40,56},{48,32},{56,40},{64,80... | collective-permute-start | bytes 589832 | tf_op jit(solution)/shard_map/ppermute | solution.py:22
  201.3 6.5 %collective-permute-start.37 = (bf16[24,4096]{1,0:T(8,128)(2,1)S(1)}, bf16[24,4096]{1,0:T(8,128)(2,1)S(1)}, u32[]{:S(2)}, u32[]{:S(2)}) collective-permute-start(bf16[24,4096]{1,0:T(8,128)(2,1)S(1)} %get-tuple-element.69), channel_id=1, source_target_pairs={{0,8},{8,16},{16,24},{24,0},{32,40},{40,48},{48,56},{56,32},{64,72... | collective-permute-start | bytes 589832 | tf_op jit(solution)/shard_map/ppermute | solution.py:22
  208.9 23.3 %all-to-all-start.2 = ((bf16[8,48,512]{2,1,0:T(8,128)(2,1)}), bf16[8,48,512]{2,1,0:T(8,128)(2,1)S(1)}, u32[]{:S(2)}, u32[]{:S(2)}) async-start(bf16[8,48,512]{2,1,0:T(8,128)(2,1)} %copy.55), calls=%async_computation.2 | async-start | bytes 786432 | tf_op jit(solution)/shard_map/all_to_all | solution.py:366
  (21 other events, 212.8 us)
where the time goes:
time: 234 us; the launch traced here: 233 us
  starting transfers between devices  81.4 us (35%)
  waiting for transfers between devices  71.6 us (31%)
  Pallas kernels  27.4 us (12%)
  matrix products  18.1 us (8%)
  blocking collectives  13.1 us (6%)
  local copies, waits for them, and re-layouts  12.6 us (5%)
  other arithmetic  8.44 us (4%)
    ppermute x42, starting transfers between devices, shift(): return lax.ppermute(value, 'seq', route)  53.2 us
    ppermute x42, waiting for transfers between devices, shift(): return lax.ppermute(value, 'seq', route)  52.5 us
    all_to_all x1, starting transfers between devices, local(): returned = lax.all_to_all(summed, 'exp', split_axis=0, concat_axis=0)  15.2 us
    all_to_all x1, blocking collectives, local(): lax.all_to_all(outgoing, 'exp', split_axis=0, concat_axis=2, tiled=True)[0]  13.1 us
    pallas_call x2, Pallas kernels, call(): pl.pallas_call(project_kernel, out_shape=[jax.ShapeDtypeStruct(shape, BF1...  11.6 us
    pallas_call x1, Pallas kernels, mixer(): pl.pallas_call(second_pass, out_shape=jax.ShapeDtypeStruct((tokens, chann...  8.47 us
    all_to_all x1, waiting for transfers between devices, project(): lax.all_to_all(partial, 'exp', split_axis=0, concat_axis=0, axis_index_gr...  8.2 us
    all_to_all x1, waiting for transfers between devices, local(): returned = lax.all_to_all(summed, 'exp', split_axis=0, concat_axis=0)  8.09 us
  transfers between devices with their start and end apart: 48, of which 23 were waited for; matrix products, arithmetic and copies ran while one was open for 10% of the time, Pallas kernels for 9%

commit v1 on v0

--- a/solution.py
+++ b/solution.py
@@ -188,7 +188,7 @@
     tokens, channels = mixer_in.shape
     count, index = lax.axis_size("seq"), lax.axis_index("seq")
     rim = lax.ppermute(mixer_in[tokens - 8 :], "seq", [(i, i + 1) for i in range(count - 1)])
-    split = 7 * channels // 16
+    split = channels // 2
     low, high = w_out[:split], w_out[split:]
     low_pair = jnp.stack([low, shift(low, "x", 2)])
     dt_raw, low_pair = lax.optimization_barrier((dt_raw, low_pair))

time: 234 us -> 235 us (level)
  other arithmetic: 8.44 us -> 11.3 us
  transfers between devices with their start and end apart: 48 -> 48, of which waited for: 23 -> 24; matrix products, arithmetic and copies ran while one was open for 10% -> 11% of each run, Pallas kernels for 9% -> 9%
where the time goes in v1:
time: 235 us; the launch traced here: 234 us
  starting transfers between devices  81.7 us (35%)
  waiting for transfers between devices  70.9 us (30%)
  Pallas kernels  26.7 us (11%)
  matrix products  18.1 us (8%)
  blocking collectives  13.1 us (6%)
  local copies, waits for them, and re-layouts  11.4 us (5%)
  other arithmetic  11.3 us (5%)
    ppermute x42, starting transfers between devices, shift(): return lax.ppermute(value, 'seq', route)  53.7 us
    ppermute x42, waiting for transfers between devices, shift(): return lax.ppermute(value, 'seq', route)  51.8 us
    all_to_all x1, starting transfers between devices, local(): returned = lax.all_to_all(summed, 'exp', split_axis=0, concat_axis=0)  15.2 us
    all_to_all x1, blocking collectives, local(): lax.all_to_all(outgoing, 'exp', split_axis=0, concat_axis=2, tiled=True)[0]  13.1 us
    pallas_call x2, Pallas kernels, call(): pl.pallas_call(project_kernel, out_shape=[jax.ShapeDtypeStruct(shape, BF1...  10.9 us
    pallas_call x1, Pallas kernels, mixer(): pl.pallas_call(second_pass, out_shape=jax.ShapeDtypeStruct((tokens, chann...  8.49 us
    all_to_all x1, waiting for transfers between devices, project(): lax.all_to_all(partial, 'exp', split_axis=0, concat_axis=0, axis_index_gr...  8.19 us
    all_to_all x1, waiting for transfers between devices, local(): returned = lax.all_to_all(summed, 'exp', split_axis=0, concat_axis=0)  8.09 us
  transfers between devices with their start and end apart: 48, of which 24 were waited for; matrix products, arithmetic and copies ran while one was open for 11% of the time, Pallas kernels for 9%

profile of v1, /device:TPU:1, one launch (start us, length us, event | category | flops | bytes accessed | tf_op | source)
XLA Modules:
  0.0 234.0 jit_solution(15238286679030949525)
XLA Ops:
  1.1 3.7 %collective-permute-start = (bf16[512,256]{1,0:T(8,128)(2,1)S(1)}, bf16[512,256]{1,0:T(8,128)(2,1)S(1)}, u32[]{:S(2)}, u32[]{:S(2)}) collective-permute-start(bf16[512,256]{1,0:T(8,128)(2,1)S(1)} %get-tuple-element.79), channel_id=1, source_target_pairs={{0,16},{8,24},{16,0},{24,8},{32,48},{40,56},{48,32},{56,40},{64,80... | collective-permute-start | bytes 786440 | tf_op jit(solution)/shard_map/ppermute | solution.py:22
  4.8 2.7 %collective-permute-start.4 = (bf16[512,256]{1,0:T(8,128)(2,1)S(1)}, bf16[512,256]{1,0:T(8,128)(2,1)S(1)}, u32[]{:S(2)}, u32[]{:S(2)}) collective-permute-start(bf16[512,256]{1,0:T(8,128)(2,1)S(1)} %get-tuple-element.29), channel_id=1, source_target_pairs={{0,96},{8,104},{16,112},{24,120},{32,0},{40,8},{48,16},{56,24},{64... | collective-permute-start | bytes 786440 | tf_op jit(solution)/shard_map/ppermute | solution.py:22
  9.2 2.2 collective-permute-start.1
  14.5 2.1 collective-permute-start.10
  18.0 7.3 %scan_state.1 = (f32[128,8,128]{2,1,0:T(8,128)}, f32[128,8,128]{2,1,0:T(8,128)}, f32[17,8,128]{2,1,0:T(8,128)}) custom-call(bf16[128,1024]{1,0:T(8,128)(2,1)} %x_hbm.1, bf16[128,1024]{1,0:T(8,128)(2,1)} %dt_hbm, bf16[8,1024]{1,0:T(8,128)(2,1)} %copy-done.11, f32[1,1024]{1,0:T(1,128)} %bitcast.267, f32[4,1024]{1,0:T(4,128)} %bitcast.266, ...), custom_call_target="tpu_custom_call" | custom-call | tf_op jit(solution)/shard_map/scan_state/pallas_call | solution.py:202
  25.3 2.2 collective-permute-start.7
  28.3 1.5 collective-permute-done.7
  30.5 2.2 collective-permute-done.6
  36.4 6.8 %collective-permute-done.8.refs_1_ = bf16[2,512,256]{2,1,0:T(8,128)(2,1)S(1)} collective-permute-done((bf16[2,512,256]{2,1,0:T(8,128)(2,1)S(1)}, bf16[2,512,256]{2,1,0:T(8,128)(2,1)S(1)}, u32[]{:S(2)}, u32[]{:S(2)}) %collective-permute-start.8) | collective-permute-done | bytes 524320 | tf_op jit(solution)/shard_map/ppermute | solution.py:22
  45.2 1.5 collective-permute-start.14
  46.9 2.3 collective-permute-done.13
  49.2 2.4 %collective-permute-done.12 = f32[17,8,128]{2,1,0:T(8,128)S(1)} collective-permute-done((f32[17,8,128]{2,1,0:T(8,128)}, f32[17,8,128]{2,1,0:T(8,128)S(1)}, u32[]{:S(2)}, u32[]{:S(2)}) %collective-permute-start.12) | collective-permute-done | bytes 69664 | tf_op jit(solution)/shard_map/ppermute | solution.py:22
  53.0 8.5 %scan_output.1.refs_6_ = bf16[128,1024]{1,0:T(8,128)(2,1)} custom-call(f32[128,8,128]{2,1,0:T(8,128)} %get-tuple-element.40.step_hbm, f32[128,8,128]{2,1,0:T(8,128)} %get-tuple-element.41.act_hbm, bf16[128,1024]{1,0:T(8,128)(2,1)} %gate_hbm.1, f32[16,8,128]{2,1,0:T(8,128)} %fusion.67.enter_ref, f32[16,8,128]{2,1,0:T(8,128)} %bitcast.240, ...), custom_call_target="tpu_custom_call" | custom-call | tf_op jit(solution)/shard_map/scan_output/pallas_call | solution.py:215
  63.5 5.2 %project.2 = (bf16[4,128,256]{2,1,0:T(8,128)(2,1)}, bf16[4,128,256]{2,1,0:T(8,128)(2,1)}) custom-call(s32[2]{0:T(128)} %pad_add_fusion.place_ref, bf16[2,512,256]{2,1,0:T(8,128)(2,1)} %copy-done.1, bf16[2,512,256]{2,1,0:T(8,128)(2,1)} %copy-done.5, bf16[2,512,256]{2,1,0:T(8,128)(2,1)} %copy-done.4, bf16[2,512,256]{2,1,0:T(8,128)(2,1)} %copy-done.3, ...), custom_call_target="tpu_custom_call" | custom-call | tf_op jit(solution)/shard_map/project/pallas_call | solution.py:262
  69.4 5.6 %project.3 = (bf16[4,2,128,256]{3,2,1,0:T(8,128)(2,1)}, bf16[4,2,128,256]{3,2,1,0:T(8,128)(2,1)}) custom-call(s32[2]{0:T(128)} %pad_add_fusion.place_ref, bf16[2,512,256]{2,1,0:T(8,128)(2,1)} %copy-done.1, bf16[2,512,256]{2,1,0:T(8,128)(2,1)} %copy-done.5, bf16[2,512,256]{2,1,0:T(8,128)(2,1)} %copy-done.4, bf16[2,512,256]{2,1,0:T(8,128)(2,1)} %copy-done.3, ...), custom_call_target="tpu_custom_call" | custom-call | tf_op jit(solution)/shard_map/project/pallas_call | solution.py:262
  75.1 4.0 %collective-permute-start.16 = (bf16[4,2,128,256]{3,2,1,0:T(8,128)(2,1)}, bf16[4,2,128,256]{3,2,1,0:T(8,128)(2,1)S(1)}, u32[]{:S(2)}, u32[]{:S(2)}) collective-permute-start(bf16[4,2,128,256]{3,2,1,0:T(8,128)(2,1)} %get-tuple-element.46), channel_id=1, source_target_pairs={{0,1},{1,0},{2,3},{3,2},{4,5},{5,4},{6,7},{7,6},{8,9},{9,8},{10,11... | collective-permute-start | bytes 1572872 | tf_op jit(solution)/shard_map/ppermute | solution.py:282
  80.8 2.0 add_convert_fusion
  82.8 5.0 %all-to-all-start = ((bf16[4,2,128,256]{3,2,1,0:T(8,128)(2,1)}), bf16[4,2,128,256]{3,2,1,0:T(8,128)(2,1)S(1)}, u32[]{:S(2)}, u32[]{:S(2)}) async-start(bf16[4,2,128,256]{3,2,1,0:T(8,128)(2,1)} %add_convert_fusion), calls=%async_computation | async-start | bytes 1048576 | tf_op jit(solution)/shard_map/all_to_all | solution.py:285
  88.6 8.2 %all-to-all-done = bf16[4,2,128,256]{3,2,1,0:T(8,128)(2,1)S(1)} async-done(((bf16[4,2,128,256]{3,2,1,0:T(8,128)(2,1)}), bf16[4,2,128,256]{3,2,1,0:T(8,128)(2,1)S(1)}, u32[]{:S(2)}, u32[]{:S(2)}) %all-to-all-start) | async-done | bytes 524320 | tf_op jit(solution)/shard_map/all_to_all | solution.py:285
  98.1 1.9 collective-permute-done.17
  100.4 13.1 %all_to_all.19 = bf16[8,48,512]{2,1,0:T(8,128)(2,1)S(1)} all-to-all(bf16[8,48,512]{2,1,0:T(8,128)(2,1)S(1)} %bitcast.245), channel_id=1, replica_groups=mesh['seq'=16,'exp'=8] {'exp'}, dimensions={0} | all-to-all | bytes 786432 | tf_op jit(solution)/shard_map/all_to_all | solution.py:338
  115.2 1.8 collective-permute-start.23
  117.1 3.9 %collective-permute-start.19 = (bf16[24,4096]{1,0:T(8,128)(2,1)S(1)}, bf16[24,4096]{1,0:T(8,128)(2,1)S(1)}, u32[]{:S(2)}, u32[]{:S(2)}) collective-permute-start(bf16[24,4096]{1,0:T(8,128)(2,1)S(1)} %get-tuple-element.83), channel_id=1, source_target_pairs={{0,16},{8,24},{16,0},{24,8},{32,48},{40,56},{48,32},{56,40},{64,80... | collective-permute-start | bytes 589832 | tf_op jit(solution)/shard_map/ppermute | solution.py:22
  121.3 2.3 collective-permute-start.20
  123.7 2.9 %collective-permute-done.21 = bf16[24,4096]{1,0:T(8,128)(2,1)S(1)} collective-permute-done((bf16[24,4096]{1,0:T(8,128)(2,1)S(1)}, bf16[24,4096]{1,0:T(8,128)(2,1)S(1)}, u32[]{:S(2)}, u32[]{:S(2)}) %collective-permute-start.21) | collective-permute-done | bytes 196640 | tf_op jit(solution)/shard_map/ppermute | solution.py:22
  129.8 2.7 %collective-permute-start.25 = (bf16[4,24,4096]{2,1,0:T(8,128)(2,1)S(1)}, bf16[4,24,4096]{2,1,0:T(8,128)(2,1)S(1)}, u32[]{:S(2)}, u32[]{:S(2)}) collective-permute-start(bf16[4,24,4096]{2,1,0:T(8,128)(2,1)S(1)} %get-tuple-element.74), channel_id=1, source_target_pairs={{0,96},{8,104},{16,112},{24,120},{32,0},{40,8},{48,16},{56,24},{64... | collective-permute-start | bytes 2359304 | tf_op jit(solution)/shard_map/ppermute | solution.py:22
  135.4 1.4 fusion.38
  138.9 7.9 %collective-permute-done.26 = bf16[4,24,4096]{2,1,0:T(8,128)(2,1)S(1)} collective-permute-done((bf16[4,24,4096]{2,1,0:T(8,128)(2,1)S(1)}, bf16[4,24,4096]{2,1,0:T(8,128)(2,1)S(1)}, u32[]{:S(2)}, u32[]{:S(2)}) %collective-permute-start.26) | collective-permute-done | bytes 786464 | tf_op jit(solution)/shard_map/ppermute | solution.py:22
  147.8 2.0 collective-permute-start.31
  149.9 2.9 %collective-permute-start.29 = (bf16[2,24,4096]{2,1,0:T(8,128)(2,1)S(1)}, bf16[2,24,4096]{2,1,0:T(8,128)(2,1)S(1)}, u32[]{:S(2)}, u32[]{:S(2)}) collective-permute-start(bf16[2,24,4096]{2,1,0:T(8,128)(2,1)S(1)} %slice.305), channel_id=1, source_target_pairs={{0,96},{8,104},{16,112},{24,120},{32,0},{40,8},{48,16},{56,24},{64... | collective-permute-start | bytes 1179656 | tf_op jit(solution)/shard_map/ppermute | solution.py:22
  153.3 2.6 %fusion.14 = f32[384,768]{1,0:T(8,128)S(1)} fusion(bf16[384,4096]{1,0:T(8,128)(2,1)S(1)} %bitcast.228, bf16[1,4096,768]{2,1,0:T(8,128)(2,1)S(1)} %bitcast.271), kind=kOutput, calls=%fused_computation.14 | convolution fusion | flops 2415919104 | bytes 10616832 | tf_op jit(solution)/shard_map/dot_general | solution.py:349
  155.9 2.7 %multiply_convert_fusion = bf16[384,768]{1,0:T(8,128)(2,1)S(1)} fusion(f32[384,768]{1,0:T(8,128)S(1)} %fusion.14, bf16[384,4096]{1,0:T(8,128)(2,1)S(1)} %bitcast.229, bf16[1,4096,768]{2,1,0:T(8,128)(2,1)S(1)} %bitcast.273), kind=kOutput, calls=%fused_computation.33 | convolution fusion | flops 2417688576 | bytes 11206656 | tf_op jit(solution)/shard_map/dot_general | solution.py:350
  158.5 2.8 %fusion.18 = bf16[384,4096]{1,0:T(8,128)(2,1)S(1)} fusion(bf16[384,768]{1,0:T(8,128)(2,1)S(1)} %multiply_convert_fusion, bf16[1,768,4096]{2,1,0:T(8,128)(2,1)S(1)} %bitcast.275), kind=kOutput, calls=%fused_computation.18 | convolution fusion | flops 2417491968 | bytes 10027008 | tf_op jit(solution)/shard_map/dot_general | solution.py:352
  161.7 1.4 fusion.12
  163.2 1.4 fusion.35
  167.7 2.7 %collective-permute-start.34 = (bf16[2,24,4096]{2,1,0:T(8,128)(2,1)S(1)}, bf16[2,24,4096]{2,1,0:T(8,128)(2,1)S(1)}, u32[]{:S(2)}, u32[]{:S(2)}) collective-permute-start(bf16[2,24,4096]{2,1,0:T(8,128)(2,1)S(1)} %bitcast.251), channel_id=1, source_target_pairs={{0,96},{8,104},{16,112},{24,120},{32,0},{40,8},{48,16},{56,24},{64... | collective-permute-start | bytes 1179656 | tf_op jit(solution)/shard_map/ppermute | solution.py:22
  170.5 4.0 %collective-permute-done.41 = bf16[2,24,4096]{2,1,0:T(8,128)(2,1)S(1)} collective-permute-done((bf16[2,24,4096]{2,1,0:T(8,128)(2,1)S(1)}, bf16[2,24,4096]{2,1,0:T(8,128)(2,1)S(1)}, u32[]{:S(2)}, u32[]{:S(2)}) %collective-permute-start.41) | collective-permute-done | bytes 393248 | tf_op jit(solution)/shard_map/ppermute | solution.py:22
  177.6 1.7 collective-permute-start.42
  179.4 3.5 %collective-permute-start.35 = (bf16[4,24,4096]{2,1,0:T(8,128)(2,1)S(1)}, bf16[4,24,4096]{2,1,0:T(8,128)(2,1)S(1)}, u32[]{:S(2)}, u32[]{:S(2)}) collective-permute-start(bf16[4,24,4096]{2,1,0:T(8,128)(2,1)S(1)} %pad_maximum_fusion.7), channel_id=1, source_target_pairs={{0,96},{8,104},{16,112},{24,120},{32,0},{40,8},{48,16},{56,24},{64... | collective-permute-start | bytes 2359304 | tf_op jit(solution)/shard_map/ppermute | solution.py:22
  183.0 9.3 %collective-permute-done.40 = bf16[4,24,4096]{2,1,0:T(8,128)(2,1)S(1)} collective-permute-done((bf16[4,24,4096]{2,1,0:T(8,128)(2,1)S(1)}, bf16[4,24,4096]{2,1,0:T(8,128)(2,1)S(1)}, u32[]{:S(2)}, u32[]{:S(2)}) %collective-permute-start.40) | collective-permute-done | bytes 786464 | tf_op jit(solution)/shard_map/ppermute | solution.py:22
  193.4 2.7 %collective-permute-start.43 = (bf16[24,4096]{1,0:T(8,128)(2,1)S(1)}, bf16[24,4096]{1,0:T(8,128)(2,1)S(1)}, u32[]{:S(2)}, u32[]{:S(2)}) collective-permute-start(bf16[24,4096]{1,0:T(8,128)(2,1)S(1)} %get-tuple-element.70), channel_id=1, source_target_pairs={{0,96},{8,104},{16,112},{24,120},{32,0},{40,8},{48,16},{56,24},{64... | collective-permute-start | bytes 589832 | tf_op jit(solution)/shard_map/ppermute | solution.py:22
  198.6 1.4 collective-permute-start.36
  200.1 1.8 collective-permute-done.43
  201.9 2.3 collective-permute-done.45
  204.2 2.5 %collective-permute-done.44 = bf16[24,4096]{1,0:T(8,128)(2,1)S(1)} collective-permute-done((bf16[24,4096]{1,0:T(8,128)(2,1)S(1)}, bf16[24,4096]{1,0:T(8,128)(2,1)S(1)}, u32[]{:S(2)}, u32[]{:S(2)}) %collective-permute-start.44) | collective-permute-done | bytes 196640 | tf_op jit(solution)/shard_map/ppermute | solution.py:22
  206.9 1.6 collective-permute-done.37
  209.6 15.2 %all-to-all-start.2 = ((bf16[8,48,512]{2,1,0:T(8,128)(2,1)}), bf16[8,48,512]{2,1,0:T(8,128)(2,1)S(1)}, u32[]{:S(2)}, u32[]{:S(2)}) async-start(bf16[8,48,512]{2,1,0:T(8,128)(2,1)} %copy.55), calls=%async_computation.2 | async-start | bytes 786432 | tf_op jit(solution)/shard_map/all_to_all | solution.py:366
  224.7 8.1 %all-to-all-done.2 = bf16[8,48,512]{2,1,0:T(8,128)(2,1)S(1)} async-done(((bf16[8,48,512]{2,1,0:T(8,128)(2,1)}), bf16[8,48,512]{2,1,0:T(8,128)(2,1)S(1)}, u32[]{:S(2)}, u32[]{:S(2)}) %all-to-all-start.2) | async-done | bytes 393248 | tf_op jit(solution)/shard_map/all_to_all | solution.py:366
  (178 shorter events, 47.2 us)
Async XLA Ops:
  1.1 13.3 %collective-permute-start = (bf16[512,256]{1,0:T(8,128)(2,1)S(1)}, bf16[512,256]{1,0:T(8,128)(2,1)S(1)}, u32[]{:S(2)}, u32[]{:S(2)}) collective-permute-start(bf16[512,256]{1,0:T(8,128)(2,1)S(1)} %get-tuple-element.79), channel_id=1, source_target_pairs={{0,16},{8,24},{16,0},{24,8},{32,48},{40,56},{48,32},{56,40},{64,80... | collective-permute-start | bytes 786440 | tf_op jit(solution)/shard_map/ppermute | solution.py:22
  4.8 20.6 %collective-permute-start.4 = (bf16[512,256]{1,0:T(8,128)(2,1)S(1)}, bf16[512,256]{1,0:T(8,128)(2,1)S(1)}, u32[]{:S(2)}, u32[]{:S(2)}) collective-permute-start(bf16[512,256]{1,0:T(8,128)(2,1)S(1)} %get-tuple-element.29), channel_id=1, source_target_pairs={{0,96},{8,104},{16,112},{24,120},{32,0},{40,8},{48,16},{56,24},{64... | collective-permute-start | bytes 786440 | tf_op jit(solution)/shard_map/ppermute | solution.py:22
  7.5 17.8 %collective-permute-start.3 = (bf16[512,256]{1,0:T(8,128)(2,1)S(1)}, bf16[512,256]{1,0:T(8,128)(2,1)S(1)}, u32[]{:S(2)}, u32[]{:S(2)}) collective-permute-start(bf16[512,256]{1,0:T(8,128)(2,1)S(1)} %get-tuple-element.29), channel_id=1, source_target_pairs={{0,64},{8,72},{16,80},{24,88},{32,96},{40,104},{48,112},{56,120},{... | collective-permute-start | bytes 786440 | tf_op jit(solution)/shard_map/ppermute | solution.py:22
  7.8 17.5 %collective-permute-start.2 = (bf16[512,256]{1,0:T(8,128)(2,1)S(1)}, bf16[512,256]{1,0:T(8,128)(2,1)S(1)}, u32[]{:S(2)}, u32[]{:S(2)}) collective-permute-start(bf16[512,256]{1,0:T(8,128)(2,1)S(1)} %get-tuple-element.29), channel_id=1, source_target_pairs={{0,32},{8,40},{16,48},{24,56},{32,64},{40,72},{48,80},{56,88},{64,... | collective-permute-start | bytes 786440 | tf_op jit(solution)/shard_map/ppermute | solution.py:22
  9.2 7.3 %collective-permute-start.1 = (bf16[8,1024]{1,0:T(8,128)(2,1)S(1)}, bf16[8,1024]{1,0:T(8,128)(2,1)S(1)}, u32[]{:S(2)}, u32[]{:S(2)}) collective-permute-start(bf16[8,1024]{1,0:T(8,128)(2,1)S(1)} %slice.227), channel_id=1, source_target_pairs={{0,8},{8,16},{16,24},{24,32},{32,40},{40,48},{48,56},{56,64},{64,7... | collective-permute-start | bytes 49160 | tf_op jit(solution)/shard_map/ppermute | solution.py:190
  14.5 21.9 %collective-permute-start.10 = (bf16[2,512,256]{2,1,0:T(8,128)(2,1)S(1)}, bf16[2,512,256]{2,1,0:T(8,128)(2,1)S(1)}, u32[]{:S(2)}, u32[]{:S(2)}) collective-permute-start(bf16[2,512,256]{2,1,0:T(8,128)(2,1)S(1)} %pad_maximum_fusion.10.refs_0_), channel_id=1, source_target_pairs={{0,96},{8,104},{16,112},{24,120},{32,0},{40,8},{48,16},{56,24},{64... | collective-permute-start | bytes 1572872 | tf_op jit(solution)/shard_map/ppermute | solution.py:22
  16.6 19.9 %collective-permute-start.9 = (bf16[2,512,256]{2,1,0:T(8,128)(2,1)S(1)}, bf16[2,512,256]{2,1,0:T(8,128)(2,1)S(1)}, u32[]{:S(2)}, u32[]{:S(2)}) collective-permute-start(bf16[2,512,256]{2,1,0:T(8,128)(2,1)S(1)} %pad_maximum_fusion.10.refs_0_), channel_id=1, source_target_pairs={{0,64},{8,72},{16,80},{24,88},{32,96},{40,104},{48,112},{56,120},{... | collective-permute-start | bytes 1572872 | tf_op jit(solution)/shard_map/ppermute | solution.py:22
  25.3 4.5 %collective-permute-start.7 = (f32[17,8,128]{2,1,0:T(8,128)}, f32[17,8,128]{2,1,0:T(8,128)S(1)}, u32[]{:S(2)}, u32[]{:S(2)}) collective-permute-start(f32[17,8,128]{2,1,0:T(8,128)} %get-tuple-element.28), channel_id=1, source_target_pairs={{0,24},{8,0},{16,8},{24,16},{32,56},{40,32},{48,40},{56,48},{64,88... | collective-permute-start | bytes 208904 | tf_op jit(solution)/shard_map/ppermute | solution.py:22
  27.5 5.2 %collective-permute-start.6 = (f32[17,8,128]{2,1,0:T(8,128)}, f32[17,8,128]{2,1,0:T(8,128)S(1)}, u32[]{:S(2)}, u32[]{:S(2)}) collective-permute-start(f32[17,8,128]{2,1,0:T(8,128)} %get-tuple-element.28), channel_id=1, source_target_pairs={{0,16},{8,24},{16,0},{24,8},{32,48},{40,56},{48,32},{56,40},{64,80... | collective-permute-start | bytes 208904 | tf_op jit(solution)/shard_map/ppermute | solution.py:22
  27.5 5.6 %collective-permute-start.5 = (f32[17,8,128]{2,1,0:T(8,128)}, f32[17,8,128]{2,1,0:T(8,128)S(1)}, u32[]{:S(2)}, u32[]{:S(2)}) collective-permute-start(f32[17,8,128]{2,1,0:T(8,128)} %get-tuple-element.28), channel_id=1, source_target_pairs={{0,8},{8,16},{16,24},{24,0},{32,40},{40,48},{48,56},{56,32},{64,72... | collective-permute-start | bytes 208904 | tf_op jit(solution)/shard_map/ppermute | solution.py:22
  29.8 13.4 %collective-permute-start.8 = (bf16[2,512,256]{2,1,0:T(8,128)(2,1)S(1)}, bf16[2,512,256]{2,1,0:T(8,128)(2,1)S(1)}, u32[]{:S(2)}, u32[]{:S(2)}) collective-permute-start(bf16[2,512,256]{2,1,0:T(8,128)(2,1)S(1)} %pad_maximum_fusion.10.refs_0_), channel_id=1, source_target_pairs={{0,32},{8,40},{16,48},{24,56},{32,64},{40,72},{48,80},{56,88},{64,... | collective-permute-start | bytes 1572872 | tf_op jit(solution)/shard_map/ppermute | solution.py:22
  35.4 27.0 %collective-permute-start.11 = (bf16[4,512,256]{2,1,0:T(8,128)(2,1)S(1)}, bf16[4,512,256]{2,1,0:T(8,128)(2,1)S(1)}, u32[]{:S(2)}, u32[]{:S(2)}) collective-permute-start(bf16[4,512,256]{2,1,0:T(8,128)(2,1)S(1)} %pad_maximum_fusion.3.refs_4_), channel_id=1, source_target_pairs={{0,16},{8,24},{16,0},{24,8},{32,48},{40,56},{48,32},{56,40},{64,80... | collective-permute-start | bytes 3145736 | tf_op jit(solution)/shard_map/ppermute | solution.py:22
  44.0 5.2 %collective-permute-start.13 = (f32[17,8,128]{2,1,0:T(8,128)}, f32[17,8,128]{2,1,0:T(8,128)S(1)}, u32[]{:S(2)}, u32[]{:S(2)}) collective-permute-start(f32[17,8,128]{2,1,0:T(8,128)} %pad_maximum_fusion.11), channel_id=1, source_target_pairs={{0,64},{8,72},{16,80},{24,88},{32,96},{40,104},{48,112},{56,120},{... | collective-permute-start | bytes 208904 | tf_op jit(solution)/shard_map/ppermute | solution.py:22
  45.2 6.4 %collective-permute-start.14 = (f32[17,8,128]{2,1,0:T(8,128)}, f32[17,8,128]{2,1,0:T(8,128)S(1)}, u32[]{:S(2)}, u32[]{:S(2)}) collective-permute-start(f32[17,8,128]{2,1,0:T(8,128)} %pad_maximum_fusion.11), channel_id=1, source_target_pairs={{0,96},{8,104},{16,112},{24,120},{32,0},{40,8},{48,16},{56,24},{64... | collective-permute-start | bytes 208904 | tf_op jit(solution)/shard_map/ppermute | solution.py:22
  46.7 4.9 %collective-permute-start.12 = (f32[17,8,128]{2,1,0:T(8,128)}, f32[17,8,128]{2,1,0:T(8,128)S(1)}, u32[]{:S(2)}, u32[]{:S(2)}) collective-permute-start(f32[17,8,128]{2,1,0:T(8,128)} %pad_maximum_fusion.11), channel_id=1, source_target_pairs={{0,32},{8,40},{16,48},{24,56},{32,64},{40,72},{48,80},{56,88},{64,... | collective-permute-start | bytes 208904 | tf_op jit(solution)/shard_map/ppermute | solution.py:22
  61.5 7.2 %collective-permute-start.15 = (bf16[128,1024]{1,0:T(8,128)(2,1)}, bf16[128,1024]{1,0:T(8,128)(2,1)S(1)}, u32[]{:S(2)}, u32[]{:S(2)}) collective-permute-start(bf16[128,1024]{1,0:T(8,128)(2,1)} %scan_output.1.refs_6_), channel_id=1, source_target_pairs={{0,8},{8,0},{16,24},{24,16},{32,40},{40,32},{48,56},{56,48},{64,72... | collective-permute-start | bytes 786440 | tf_op jit(solution)/shard_map/ppermute | solution.py:27
  75.1 5.7 %collective-permute-start.16 = (bf16[4,2,128,256]{3,2,1,0:T(8,128)(2,1)}, bf16[4,2,128,256]{3,2,1,0:T(8,128)(2,1)S(1)}, u32[]{:S(2)}, u32[]{:S(2)}) collective-permute-start(bf16[4,2,128,256]{3,2,1,0:T(8,128)(2,1)} %get-tuple-element.46), channel_id=1, source_target_pairs={{0,1},{1,0},{2,3},{3,2},{4,5},{5,4},{6,7},{7,6},{8,9},{9,8},{10,11... | collective-permute-start | bytes 1572872 | tf_op jit(solution)/shard_map/ppermute | solution.py:282
  82.8 13.9 %all-to-all-start = ((bf16[4,2,128,256]{3,2,1,0:T(8,128)(2,1)}), bf16[4,2,128,256]{3,2,1,0:T(8,128)(2,1)S(1)}, u32[]{:S(2)}, u32[]{:S(2)}) async-start(bf16[4,2,128,256]{3,2,1,0:T(8,128)(2,1)} %add_convert_fusion), calls=%async_computation | async-start | bytes 1048576 | tf_op jit(solution)/shard_map/all_to_all | solution.py:285
  96.9 3.2 %collective-permute-start.17 = (bf16[128,256]{1,0:T(8,128)(2,1)S(1)}, bf16[128,256]{1,0:T(8,128)(2,1)S(1)}, u32[]{:S(2)}, u32[]{:S(2)}) collective-permute-start(bf16[128,256]{1,0:T(8,128)(2,1)S(1)} %fusion.64), channel_id=1, source_target_pairs={{0,8},{8,0},{16,24},{24,16},{32,40},{40,32},{48,56},{56,48},{64,72... | collective-permute-start | bytes 196616 | tf_op jit(solution)/shard_map/ppermute | solution.py:27
  114.1 7.2 %collective-permute-start.22 = (bf16[24,4096]{1,0:T(8,128)(2,1)S(1)}, bf16[24,4096]{1,0:T(8,128)(2,1)S(1)}, u32[]{:S(2)}, u32[]{:S(2)}) collective-permute-start(bf16[24,4096]{1,0:T(8,128)(2,1)S(1)} %get-tuple-element.82), channel_id=1, source_target_pairs={{0,64},{8,72},{16,80},{24,88},{32,96},{40,104},{48,112},{56,120},{... | collective-permute-start | bytes 589832 | tf_op jit(solution)/shard_map/ppermute | solution.py:22
  114.4 12.1 %collective-permute-start.21 = (bf16[24,4096]{1,0:T(8,128)(2,1)S(1)}, bf16[24,4096]{1,0:T(8,128)(2,1)S(1)}, u32[]{:S(2)}, u32[]{:S(2)}) collective-permute-start(bf16[24,4096]{1,0:T(8,128)(2,1)S(1)} %get-tuple-element.82), channel_id=1, source_target_pairs={{0,32},{8,40},{16,48},{24,56},{32,64},{40,72},{48,80},{56,88},{64,... | collective-permute-start | bytes 589832 | tf_op jit(solution)/shard_map/ppermute | solution.py:22
  115.2 11.3 %collective-permute-start.23 = (bf16[24,4096]{1,0:T(8,128)(2,1)S(1)}, bf16[24,4096]{1,0:T(8,128)(2,1)S(1)}, u32[]{:S(2)}, u32[]{:S(2)}) collective-permute-start(bf16[24,4096]{1,0:T(8,128)(2,1)S(1)} %get-tuple-element.82), channel_id=1, source_target_pairs={{0,96},{8,104},{16,112},{24,120},{32,0},{40,8},{48,16},{56,24},{64... | collective-permute-start | bytes 589832 | tf_op jit(solution)/shard_map/ppermute | solution.py:22
  117.1 12.4 %collective-permute-start.19 = (bf16[24,4096]{1,0:T(8,128)(2,1)S(1)}, bf16[24,4096]{1,0:T(8,128)(2,1)S(1)}, u32[]{:S(2)}, u32[]{:S(2)}) collective-permute-start(bf16[24,4096]{1,0:T(8,128)(2,1)S(1)} %get-tuple-element.83), channel_id=1, source_target_pairs={{0,16},{8,24},{16,0},{24,8},{32,48},{40,56},{48,32},{56,40},{64,80... | collective-permute-start | bytes 589832 | tf_op jit(solution)/shard_map/ppermute | solution.py:22
  121.0 8.6 %collective-permute-start.18 = (bf16[24,4096]{1,0:T(8,128)(2,1)S(1)}, bf16[24,4096]{1,0:T(8,128)(2,1)S(1)}, u32[]{:S(2)}, u32[]{:S(2)}) collective-permute-start(bf16[24,4096]{1,0:T(8,128)(2,1)S(1)} %get-tuple-element.83), channel_id=1, source_target_pairs={{0,8},{8,16},{16,24},{24,0},{32,40},{40,48},{48,56},{56,32},{64,72... | collective-permute-start | bytes 589832 | tf_op jit(solution)/shard_map/ppermute | solution.py:22
  121.3 8.2 %collective-permute-start.20 = (bf16[24,4096]{1,0:T(8,128)(2,1)S(1)}, bf16[24,4096]{1,0:T(8,128)(2,1)S(1)}, u32[]{:S(2)}, u32[]{:S(2)}) collective-permute-start(bf16[24,4096]{1,0:T(8,128)(2,1)S(1)} %get-tuple-element.83), channel_id=1, source_target_pairs={{0,24},{8,0},{16,8},{24,16},{32,56},{40,32},{48,40},{56,48},{64,88... | collective-permute-start | bytes 589832 | tf_op jit(solution)/shard_map/ppermute | solution.py:22
  126.7 20.2 %collective-permute-start.26 = (bf16[4,24,4096]{2,1,0:T(8,128)(2,1)S(1)}, bf16[4,24,4096]{2,1,0:T(8,128)(2,1)S(1)}, u32[]{:S(2)}, u32[]{:S(2)}) collective-permute-start(bf16[4,24,4096]{2,1,0:T(8,128)(2,1)S(1)} %get-tuple-element.76), channel_id=1, source_target_pairs={{0,8},{8,16},{16,24},{24,0},{32,40},{40,48},{48,56},{56,32},{64,72... | collective-permute-start | bytes 2359304 | tf_op jit(solution)/shard_map/ppermute | solution.py:22
  128.0 19.7 %collective-permute-start.27 = (bf16[4,24,4096]{2,1,0:T(8,128)(2,1)S(1)}, bf16[4,24,4096]{2,1,0:T(8,128)(2,1)S(1)}, u32[]{:S(2)}, u32[]{:S(2)}) collective-permute-start(bf16[4,24,4096]{2,1,0:T(8,128)(2,1)S(1)} %get-tuple-element.76), channel_id=1, source_target_pairs={{0,24},{8,0},{16,8},{24,16},{32,56},{40,32},{48,40},{56,48},{64,88... | collective-permute-start | bytes 2359304 | tf_op jit(solution)/shard_map/ppermute | solution.py:22
  129.7 20.0 %collective-permute-start.24 = (bf16[4,24,4096]{2,1,0:T(8,128)(2,1)S(1)}, bf16[4,24,4096]{2,1,0:T(8,128)(2,1)S(1)}, u32[]{:S(2)}, u32[]{:S(2)}) collective-permute-start(bf16[4,24,4096]{2,1,0:T(8,128)(2,1)S(1)} %get-tuple-element.74), channel_id=1, source_target_pairs={{0,32},{8,40},{16,48},{24,56},{32,64},{40,72},{48,80},{56,88},{64,... | collective-permute-start | bytes 2359304 | tf_op jit(solution)/shard_map/ppermute | solution.py:22
  129.8 20.1 %collective-permute-start.25 = (bf16[4,24,4096]{2,1,0:T(8,128)(2,1)S(1)}, bf16[4,24,4096]{2,1,0:T(8,128)(2,1)S(1)}, u32[]{:S(2)}, u32[]{:S(2)}) collective-permute-start(bf16[4,24,4096]{2,1,0:T(8,128)(2,1)S(1)} %get-tuple-element.74), channel_id=1, source_target_pairs={{0,96},{8,104},{16,112},{24,120},{32,0},{40,8},{48,16},{56,24},{64... | collective-permute-start | bytes 2359304 | tf_op jit(solution)/shard_map/ppermute | solution.py:22
  146.9 14.5 %collective-permute-start.30 = (bf16[2,24,4096]{2,1,0:T(8,128)(2,1)S(1)}, bf16[2,24,4096]{2,1,0:T(8,128)(2,1)S(1)}, u32[]{:S(2)}, u32[]{:S(2)}) collective-permute-start(bf16[2,24,4096]{2,1,0:T(8,128)(2,1)S(1)} %slice.306), channel_id=1, source_target_pairs={{0,8},{8,16},{16,24},{24,0},{32,40},{40,48},{48,56},{56,32},{64,72... | collective-permute-start | bytes 1179656 | tf_op jit(solution)/shard_map/ppermute | solution.py:22
  147.8 13.6 %collective-permute-start.31 = (bf16[2,24,4096]{2,1,0:T(8,128)(2,1)S(1)}, bf16[2,24,4096]{2,1,0:T(8,128)(2,1)S(1)}, u32[]{:S(2)}, u32[]{:S(2)}) collective-permute-start(bf16[2,24,4096]{2,1,0:T(8,128)(2,1)S(1)} %slice.307), channel_id=1, source_target_pairs={{0,24},{8,0},{16,8},{24,16},{32,56},{40,32},{48,40},{56,48},{64,88... | collective-permute-start | bytes 1179656 | tf_op jit(solution)/shard_map/ppermute | solution.py:22
  149.8 11.7 %collective-permute-start.28 = (bf16[2,24,4096]{2,1,0:T(8,128)(2,1)S(1)}, bf16[2,24,4096]{2,1,0:T(8,128)(2,1)S(1)}, u32[]{:S(2)}, u32[]{:S(2)}) collective-permute-start(bf16[2,24,4096]{2,1,0:T(8,128)(2,1)S(1)} %slice.304), channel_id=1, source_target_pairs={{0,32},{8,40},{16,48},{24,56},{32,64},{40,72},{48,80},{56,88},{64,... | collective-permute-start | bytes 1179656 | tf_op jit(solution)/shard_map/ppermute | solution.py:22
  149.9 11.6 %collective-permute-start.29 = (bf16[2,24,4096]{2,1,0:T(8,128)(2,1)S(1)}, bf16[2,24,4096]{2,1,0:T(8,128)(2,1)S(1)}, u32[]{:S(2)}, u32[]{:S(2)}) collective-permute-start(bf16[2,24,4096]{2,1,0:T(8,128)(2,1)S(1)} %slice.305), channel_id=1, source_target_pairs={{0,96},{8,104},{16,112},{24,120},{32,0},{40,8},{48,16},{56,24},{64... | collective-permute-start | bytes 1179656 | tf_op jit(solution)/shard_map/ppermute | solution.py:22
  166.1 8.3 %collective-permute-start.41 = (bf16[2,24,4096]{2,1,0:T(8,128)(2,1)S(1)}, bf16[2,24,4096]{2,1,0:T(8,128)(2,1)S(1)}, u32[]{:S(2)}, u32[]{:S(2)}) collective-permute-start(bf16[2,24,4096]{2,1,0:T(8,128)(2,1)S(1)} %bitcast.254), channel_id=1, source_target_pairs={{0,24},{8,0},{16,8},{24,16},{32,56},{40,32},{48,40},{56,48},{64,88... | collective-permute-start | bytes 1179656 | tf_op jit(solution)/shard_map/ppermute | solution.py:22
  166.4 8.4 %collective-permute-start.32 = (bf16[2,24,4096]{2,1,0:T(8,128)(2,1)S(1)}, bf16[2,24,4096]{2,1,0:T(8,128)(2,1)S(1)}, u32[]{:S(2)}, u32[]{:S(2)}) collective-permute-start(bf16[2,24,4096]{2,1,0:T(8,128)(2,1)S(1)} %bitcast.253), channel_id=1, source_target_pairs={{0,32},{8,40},{16,48},{24,56},{32,64},{40,72},{48,80},{56,88},{64,... | collective-permute-start | bytes 1179656 | tf_op jit(solution)/shard_map/ppermute | solution.py:22
  166.4 8.4 %collective-permute-start.39 = (bf16[2,24,4096]{2,1,0:T(8,128)(2,1)S(1)}, bf16[2,24,4096]{2,1,0:T(8,128)(2,1)S(1)}, u32[]{:S(2)}, u32[]{:S(2)}) collective-permute-start(bf16[2,24,4096]{2,1,0:T(8,128)(2,1)S(1)} %bitcast.252), channel_id=1, source_target_pairs={{0,8},{8,16},{16,24},{24,0},{32,40},{40,48},{48,56},{56,32},{64,72... | collective-permute-start | bytes 1179656 | tf_op jit(solution)/shard_map/ppermute | solution.py:22
  167.7 7.9 %collective-permute-start.34 = (bf16[2,24,4096]{2,1,0:T(8,128)(2,1)S(1)}, bf16[2,24,4096]{2,1,0:T(8,128)(2,1)S(1)}, u32[]{:S(2)}, u32[]{:S(2)}) collective-permute-start(bf16[2,24,4096]{2,1,0:T(8,128)(2,1)S(1)} %bitcast.251), channel_id=1, source_target_pairs={{0,96},{8,104},{16,112},{24,120},{32,0},{40,8},{48,16},{56,24},{64... | collective-permute-start | bytes 1179656 | tf_op jit(solution)/shard_map/ppermute | solution.py:22
  176.2 16.2 %collective-permute-start.40 = (bf16[4,24,4096]{2,1,0:T(8,128)(2,1)S(1)}, bf16[4,24,4096]{2,1,0:T(8,128)(2,1)S(1)}, u32[]{:S(2)}, u32[]{:S(2)}) collective-permute-start(bf16[4,24,4096]{2,1,0:T(8,128)(2,1)S(1)} %pad_maximum_fusion.8), channel_id=1, source_target_pairs={{0,8},{8,16},{16,24},{24,0},{32,40},{40,48},{48,56},{56,32},{64,72... | collective-permute-start | bytes 2359304 | tf_op jit(solution)/shard_map/ppermute | solution.py:22
  177.6 15.5 %collective-permute-start.42 = (bf16[4,24,4096]{2,1,0:T(8,128)(2,1)S(1)}, bf16[4,24,4096]{2,1,0:T(8,128)(2,1)S(1)}, u32[]{:S(2)}, u32[]{:S(2)}) collective-permute-start(bf16[4,24,4096]{2,1,0:T(8,128)(2,1)S(1)} %pad_maximum_fusion.9), channel_id=1, source_target_pairs={{0,24},{8,0},{16,8},{24,16},{32,56},{40,32},{48,40},{56,48},{64,88... | collective-permute-start | bytes 2359304 | tf_op jit(solution)/shard_map/ppermute | solution.py:22
  179.4 17.5 %collective-permute-start.35 = (bf16[4,24,4096]{2,1,0:T(8,128)(2,1)S(1)}, bf16[4,24,4096]{2,1,0:T(8,128)(2,1)S(1)}, u32[]{:S(2)}, u32[]{:S(2)}) collective-permute-start(bf16[4,24,4096]{2,1,0:T(8,128)(2,1)S(1)} %pad_maximum_fusion.7), channel_id=1, source_target_pairs={{0,96},{8,104},{16,112},{24,120},{32,0},{40,8},{48,16},{56,24},{64... | collective-permute-start | bytes 2359304 | tf_op jit(solution)/shard_map/ppermute | solution.py:22
  182.9 15.3 %collective-permute-start.33 = (bf16[4,24,4096]{2,1,0:T(8,128)(2,1)S(1)}, bf16[4,24,4096]{2,1,0:T(8,128)(2,1)S(1)}, u32[]{:S(2)}, u32[]{:S(2)}) collective-permute-start(bf16[4,24,4096]{2,1,0:T(8,128)(2,1)S(1)} %pad_maximum_fusion.6), channel_id=1, source_target_pairs={{0,32},{8,40},{16,48},{24,56},{32,64},{40,72},{48,80},{56,88},{64,... | collective-permute-start | bytes 2359304 | tf_op jit(solution)/shard_map/ppermute | solution.py:22
  193.4 8.5 %collective-permute-start.43 = (bf16[24,4096]{1,0:T(8,128)(2,1)S(1)}, bf16[24,4096]{1,0:T(8,128)(2,1)S(1)}, u32[]{:S(2)}, u32[]{:S(2)}) collective-permute-start(bf16[24,4096]{1,0:T(8,128)(2,1)S(1)} %get-tuple-element.70), channel_id=1, source_target_pairs={{0,96},{8,104},{16,112},{24,120},{32,0},{40,8},{48,16},{56,24},{64... | collective-permute-start | bytes 589832 | tf_op jit(solution)/shard_map/ppermute | solution.py:22
  196.2 8.1 %collective-permute-start.45 = (bf16[24,4096]{1,0:T(8,128)(2,1)S(1)}, bf16[24,4096]{1,0:T(8,128)(2,1)S(1)}, u32[]{:S(2)}, u32[]{:S(2)}) collective-permute-start(bf16[24,4096]{1,0:T(8,128)(2,1)S(1)} %get-tuple-element.71), channel_id=1, source_target_pairs={{0,64},{8,72},{16,80},{24,88},{32,96},{40,104},{48,112},{56,120},{... | collective-permute-start | bytes 589832 | tf_op jit(solution)/shard_map/ppermute | solution.py:22
  196.2 10.5 %collective-permute-start.44 = (bf16[24,4096]{1,0:T(8,128)(2,1)S(1)}, bf16[24,4096]{1,0:T(8,128)(2,1)S(1)}, u32[]{:S(2)}, u32[]{:S(2)}) collective-permute-start(bf16[24,4096]{1,0:T(8,128)(2,1)S(1)} %get-tuple-element.72), channel_id=1, source_target_pairs={{0,32},{8,40},{16,48},{24,56},{32,64},{40,72},{48,80},{56,88},{64,... | collective-permute-start | bytes 589832 | tf_op jit(solution)/shard_map/ppermute | solution.py:22
  198.6 8.2 %collective-permute-start.36 = (bf16[24,4096]{1,0:T(8,128)(2,1)S(1)}, bf16[24,4096]{1,0:T(8,128)(2,1)S(1)}, u32[]{:S(2)}, u32[]{:S(2)}) collective-permute-start(bf16[24,4096]{1,0:T(8,128)(2,1)S(1)} %get-tuple-element.67), channel_id=1, source_target_pairs={{0,24},{8,0},{16,8},{24,16},{32,56},{40,32},{48,40},{56,48},{64,88... | collective-permute-start | bytes 589832 | tf_op jit(solution)/shard_map/ppermute | solution.py:22
  200.1 6.8 %collective-permute-start.38 = (bf16[24,4096]{1,0:T(8,128)(2,1)S(1)}, bf16[24,4096]{1,0:T(8,128)(2,1)S(1)}, u32[]{:S(2)}, u32[]{:S(2)}) collective-permute-start(bf16[24,4096]{1,0:T(8,128)(2,1)S(1)} %get-tuple-element.68), channel_id=1, source_target_pairs={{0,16},{8,24},{16,0},{24,8},{32,48},{40,56},{48,32},{56,40},{64,80... | collective-permute-start | bytes 589832 | tf_op jit(solution)/shard_map/ppermute | solution.py:22
  201.9 6.6 %collective-permute-start.37 = (bf16[24,4096]{1,0:T(8,128)(2,1)S(1)}, bf16[24,4096]{1,0:T(8,128)(2,1)S(1)}, u32[]{:S(2)}, u32[]{:S(2)}) collective-permute-start(bf16[24,4096]{1,0:T(8,128)(2,1)S(1)} %get-tuple-element.69), channel_id=1, source_target_pairs={{0,8},{8,16},{16,24},{24,0},{32,40},{40,48},{48,56},{56,32},{64,72... | collective-permute-start | bytes 589832 | tf_op jit(solution)/shard_map/ppermute | solution.py:22
  209.6 23.2 %all-to-all-start.2 = ((bf16[8,48,512]{2,1,0:T(8,128)(2,1)}), bf16[8,48,512]{2,1,0:T(8,128)(2,1)S(1)}, u32[]{:S(2)}, u32[]{:S(2)}) async-start(bf16[8,48,512]{2,1,0:T(8,128)(2,1)} %copy.55), calls=%async_computation.2 | async-start | bytes 786432 | tf_op jit(solution)/shard_map/all_to_all | solution.py:366
  (21 other events, 306.9 us)
